TPU v7x, 256 devices: a whole 4x4x8 slice. The times are simulated.
256 devices in a mesh: row: 8 (over y, core), col: 32 (over z, x).
Axes of the slice: x: 4, y: 4, z: 8, core: 2. Of those that a mesh axis runs over, the one named last changes fastest.
Arguments:
- row_points: float32 [64, 16384], P(None, 'row'), may hold values from -6 to 6
- panel_points: float32 [64, 1024], P(None, 'col'), may hold values from -6 to 6
- scales: float32 [64], replicated, may hold values from 0.005 to 0.03
Outputs:
- diag_factor: float32 [1024, 1024], P('row', 'col')
- panel_factor_t: float32 [1024, 16384], P('col', 'row')
- updated_ahead_t: float32 [1024, 16384], P('col', 'row')
All inputs are finite; a program needn't handle non-finite values.
Results may differ from a plain program's by a relative error of at most 0.0003.
Values sent between devices are 32-bit elements; how exact they have to be, the bound alone decides.
No kernel may reach another device: no remote copies, remote signals or barrier semaphores. Data moves between devices by JAX's collectives and lax.ppermute only.
A program may use at most 128 MiB of HBM per device.

v0:
```python
import jax
import jax.numpy as jnp
from jax import lax
from jax.sharding import PartitionSpec as P

B = 1024


RIDGE = 0.5


def spread(block, axis, holder):
    block = jnp.where(lax.axis_index(axis) == holder, block, jnp.zeros_like(block))
    return lax.psum(block, axis)


def kernel_block(sources, targets, scales):
    weighted = sources * scales[:, None]
    source_sq = jnp.sum(weighted * sources, axis=0)
    target_sq = jnp.sum(targets * targets * scales[:, None], axis=0)
    cross = lax.dot_general(
        weighted,
        targets,
        (((0,), (0,)), ((), ())),
        precision=lax.Precision.HIGHEST,
        preferred_element_type=jnp.float32,
    )
    return jnp.exp(2.0 * cross - source_sq[:, None] - target_sq[None, :])


def times_left(matrix, pieces):
    return jnp.dot(
        matrix, pieces, precision=lax.Precision.HIGHEST, preferred_element_type=jnp.float32
    )


def transposed_times(matrix, pieces):
    return lax.dot_general(
        matrix,
        pieces,
        (((0,), (0,)), ((), ())),
        precision=lax.Precision.HIGHEST,
        preferred_element_type=jnp.float32,
    )


def body(row_points, panel_points, scales):
    n_col = lax.axis_size("col")
    n_row = lax.axis_size("row")
    col_index = lax.axis_index("col")
    row_index = lax.axis_index("row")
    col_share = B // n_col
    row_share = B // n_row
    rows_dev = row_points.shape[1]
    all_panel = lax.all_gather(panel_points, "col", axis=1, tiled=True)
    first_col = col_index * col_share
    root_row = first_col // rows_dev
    local_look = lax.dynamic_slice_in_dim(row_points, first_col % rows_dev, col_share, 1)
    look_points = spread(local_look, "row", root_row)
    identity = jnp.eye(B, dtype=jnp.float32)
    diag_block = kernel_block(all_panel, all_panel, scales) + RIDGE * identity
    diag_full = jnp.linalg.cholesky(diag_block)
    inverse = lax.linalg.triangular_solve(diag_full, identity, left_side=True, lower=True)
    own_inverse = lax.dynamic_slice_in_dim(inverse, first_col, col_share, 0)
    look_kernel = kernel_block(all_panel, look_points, scales)
    look_factor = times_left(inverse, look_kernel)
    look_rows = kernel_block(look_points, row_points, scales)
    own_kernel = kernel_block(panel_points, row_points, scales)
    panel_tile = times_left(own_inverse, lax.all_gather(own_kernel, "col", axis=0, tiled=True))
    reduction = transposed_times(look_factor, lax.all_gather(panel_tile, "col", axis=0, tiled=True))
    updated = look_rows - reduction
    diag_tile = lax.dynamic_slice(
        diag_full, (row_index * row_share, first_col), (row_share, col_share)
    )
    return (diag_tile, panel_tile, updated)


def solution(mesh):
    return jax.shard_map(
        body,
        mesh=mesh,
        in_specs=(P(None, "row"), P(None, "col"), P()),
        out_specs=(P("row", "col"), P("col", "row"), P("col", "row")),
        check_vma=False,
    )
```

profile of v0, /device:TPU:1, one launch (start us, length us, event | category | flops | bytes accessed | tf_op | source)
XLA Modules:
  0.0 574.0 jit_solution(7809796819884871075)
XLA Ops:
  8.1 23.8 %psum.7 = f32[64,32]{0,1:T(8,128)S(1)} all-reduce(f32[64,32]{0,1:T(8,128)S(1)} %broadcast_select_fusion), channel_id=1, replica_groups=mesh['row'=8,'col'=32] {'row'}, use_global_device_ids=true, to_apply=%region_20.21 | all-reduce | flops 2048 | bytes 16384 | tf_op jit(solution)/shard_map/psum | solution.py:14
  34.0 2.2 fusion.5
  36.3 42.3 %all_gather.9 = f32[64,1024]{0,1:T(8,128)S(1)} all-gather(f32[64,32]{0,1:T(8,128)} %param.4), channel_id=1, replica_groups=mesh['row'=8,'col'=32] {'col'}, dimensions={1}, use_global_device_ids=true | all-gather | bytes 270336 | tf_op jit(solution)/shard_map/all_gather | solution.py:55
  79.6 4.1 fusion.38
  85.7 2.7 fusion.1
  88.4 5.5 copy.6
  93.8 5.2 add_multiply_fusion
  101.1 11.7 %cholesky.222 = f32[128,128]{1,0:T(8,128)S(1)} custom-call(f32[128,128]{1,0:T(8,128)S(1)} %cholesky.577), custom_call_target="Cholesky" | custom-call | tf_op jit(solution)/shard_map/jit(cholesky)/cholesky | solution.py:62
  112.8 9.8 %custom-call.62 = f32[1,128,128]{1,2,0:T(8,128)S(1)} custom-call(f32[1,128,128]{2,1,0:T(8,128)S(1)} %get-tuple-element.77), custom_call_target="InvertDiagBlocksLowerTriangular" | custom-call | tf_op jit(solution)/shard_map/jit(cholesky)/cholesky | solution.py:62
  124.5 2.5 cholesky.254
  128.8 11.7 %cholesky.243 = f32[128,128]{1,0:T(8,128)S(1)} custom-call(f32[128,128]{1,0:T(8,128)S(1)} %cholesky.581), custom_call_target="Cholesky" | custom-call | tf_op jit(solution)/shard_map/jit(cholesky)/cholesky | solution.py:62
  142.1 10.0 %custom-call.63 = f32[1,128,128]{1,2,0:T(8,128)S(1)} custom-call(f32[1,128,128]{2,1,0:T(8,128)S(1)} %get-tuple-element.74), custom_call_target="InvertDiagBlocksLowerTriangular" | custom-call | tf_op jit(solution)/shard_map/jit(cholesky)/cholesky | solution.py:62
  153.3 2.1 convolution_subtract_fusion.6
  155.4 11.7 %cholesky.466 = f32[128,128]{1,0:T(8,128)S(1)} custom-call(f32[128,128]{1,0:T(8,128)S(1)} %cholesky.586), custom_call_target="Cholesky" | custom-call | tf_op jit(solution)/shard_map/jit(cholesky)/cholesky | solution.py:62
  167.7 9.8 %custom-call.64 = f32[1,128,128]{1,2,0:T(8,128)S(1)} custom-call(f32[1,128,128]{2,1,0:T(8,128)S(1)} %get-tuple-element.71), custom_call_target="InvertDiagBlocksLowerTriangular" | custom-call | tf_op jit(solution)/shard_map/jit(cholesky)/cholesky | solution.py:62
  178.8 2.3 convolution_subtract_fusion.7
  181.1 11.9 %cholesky.485 = f32[128,128]{1,0:T(8,128)S(1)} custom-call(f32[128,128]{1,0:T(8,128)S(1)} %cholesky.591), custom_call_target="Cholesky" | custom-call | tf_op jit(solution)/shard_map/jit(cholesky)/cholesky | solution.py:62
  193.7 9.8 %custom-call.65 = f32[1,128,128]{1,2,0:T(8,128)S(1)} custom-call(f32[1,128,128]{2,1,0:T(8,128)S(1)} %get-tuple-element.68), custom_call_target="InvertDiagBlocksLowerTriangular" | custom-call | tf_op jit(solution)/shard_map/jit(cholesky)/cholesky | solution.py:62
  204.6 2.3 convolution_subtract_fusion.8
  206.9 11.7 %cholesky.504 = f32[128,128]{1,0:T(8,128)S(1)} custom-call(f32[128,128]{1,0:T(8,128)S(1)} %cholesky.596), custom_call_target="Cholesky" | custom-call | tf_op jit(solution)/shard_map/jit(cholesky)/cholesky | solution.py:62
  219.3 9.8 %custom-call.66 = f32[1,128,128]{1,2,0:T(8,128)S(1)} custom-call(f32[1,128,128]{2,1,0:T(8,128)S(1)} %get-tuple-element.65), custom_call_target="InvertDiagBlocksLowerTriangular" | custom-call | tf_op jit(solution)/shard_map/jit(cholesky)/cholesky | solution.py:62
  230.1 2.7 convolution_subtract_fusion.9
  232.8 11.7 %cholesky.524 = f32[128,128]{1,0:T(8,128)S(1)} custom-call(f32[128,128]{1,0:T(8,128)S(1)} %cholesky.601), custom_call_target="Cholesky" | custom-call | tf_op jit(solution)/shard_map/jit(cholesky)/cholesky | solution.py:62
  245.2 9.8 %custom-call.67 = f32[1,128,128]{1,2,0:T(8,128)S(1)} custom-call(f32[1,128,128]{2,1,0:T(8,128)S(1)} %get-tuple-element.62), custom_call_target="InvertDiagBlocksLowerTriangular" | custom-call | tf_op jit(solution)/shard_map/jit(cholesky)/cholesky | solution.py:62
  255.9 2.1 convolution_subtract_fusion.10
  258.0 11.7 %cholesky.544 = f32[128,128]{1,0:T(8,128)S(1)} custom-call(f32[128,128]{1,0:T(8,128)S(1)} %cholesky.606), custom_call_target="Cholesky" | custom-call | tf_op jit(solution)/shard_map/jit(cholesky)/cholesky | solution.py:62
  270.4 10.0 %custom-call.68 = f32[1,128,128]{1,2,0:T(8,128)S(1)} custom-call(f32[1,128,128]{2,1,0:T(8,128)S(1)} %get-tuple-element.59), custom_call_target="InvertDiagBlocksLowerTriangular" | custom-call | tf_op jit(solution)/shard_map/jit(cholesky)/cholesky | solution.py:62
  283.0 11.7 %cholesky.562 = f32[128,128]{1,0:T(8,128)S(1)} custom-call(f32[128,128]{1,0:T(8,128)S(1)} %convolution_subtract_fusion.11), custom_call_target="Cholesky" | custom-call | tf_op jit(solution)/shard_map/jit(cholesky)/cholesky | solution.py:62
  305.0 6.6 %fusion = (f32[1024,1024]{1,0:T(8,128)}, f32[1024,1024]{1,0:T(8,128)}) fusion(f32[1024,1024]{1,0:T(8,128)} %get-tuple-element.57, pred[]{:T(512)S(6)} %cholesky.576), kind=kLoop, calls=%fused_computation.8 | loop fusion | flops 4194304 | bytes 12582913 | tf_op jit(solution)/shard_map/triangular_solve | solution.py:63
  311.6 23.2 %while.1 = (s32[]{:T(128)}, f32[1024,1024]{1,0:T(8,128)}, s32[8,2]{0,1:T(2,128)S(1)}, f32[8,128,128]{2,1,0:T(8,128)S(1)}, s32[]{:T(128)}) while((s32[]{:T(128)}, f32[1024,1024]{1,0:T(8,128)}, s32[8,2]{0,1:T(2,128)S(1)}, f32[8,128,128]{2,1,0:T(8,128)S(1)}, s32[]{:T(128)}) %tuple.65), condition=%wide.while_cond, body=%wide.while_body.sunk | while | flops 2 | bytes 131181 | solution.py:63
  312.2 2.3 bitcast_dynamic-update-slice_fusion.2
  315.1 2.3 bitcast_dynamic-update-slice_fusion.2
  318.0 2.3 bitcast_dynamic-update-slice_fusion.2
  320.9 2.3 bitcast_dynamic-update-slice_fusion.2
  323.8 2.3 bitcast_dynamic-update-slice_fusion.2
  326.8 2.3 bitcast_dynamic-update-slice_fusion.2
  329.7 2.3 bitcast_dynamic-update-slice_fusion.2
  332.6 2.2 bitcast_dynamic-update-slice_fusion.2
  334.8 78.8 %custom-call.69 = f32[8,128,128]{1,2,0:T(8,128)S(1)} custom-call(f32[8,128,128]{2,1,0:T(8,128)S(1)} %get-tuple-element.10), custom_call_target="InvertDiagBlocksLowerTriangular" | custom-call | tf_op jit(solution)/shard_map/triangular_solve | solution.py:63
  422.0 2.0 fusion.24
  425.6 2.2 fusion.27
  429.3 2.6 convolution_subtract_fusion.2
  433.4 2.8 convolution_subtract_fusion.1
  437.7 3.5 convolution_subtract_fusion.3
  442.7 9.0 %fusion.68 = f32[32,2048]{1,0:T(8,128)} fusion(f32[1024,2048]{1,0:T(8,128)} %all-gather.3.cloned.1.call-done, f32[1024,1024]{1,0:T(8,128)} %convolution_dynamic-update-slice_fusion, s32[]{:T(128)S(6)} %select_n.35), kind=kOutput, calls=%fused_computation.97 | convolution fusion | flops 805306368 | bytes 8781828 | tf_op jit(solution)/shard_map/dot_general | solution.py:32
  453.9 5.2 fusion.97
  459.2 99.2 %all-gather.5.cloned.1.call-done = f32[1024,2048]{1,0:T(8,128)} async-done(((f32[32,2048]{1,0:T(8,128)}), f32[1024,2048]{1,0:T(8,128)}) %all-gather.5.cloned.1.call-update) | async-done | bytes 8388624 | tf_op jit(solution)/shard_map/all_gather | solution.py:70
  558.3 7.2 %fusion.98 = f32[32,2048]{1,0:T(8,128)S(1)} fusion(f32[1024,32]{1,0:T(8,128)S(1)} %fusion.97, f32[1024,2048]{1,0:T(8,128)} %all-gather.5.cloned.1.call-done), kind=kOutput, calls=%fused_computation.199 | convolution fusion | flops 805306368 | bytes 8781824 | tf_op jit(solution)/shard_map/dot_general | solution.py:38
  (87 shorter events, 53.6 us)
Async XLA Ops:
  7.2 435.5 %all-gather.3.cloned.1.call-start = ((), (), s32[]{:S(2)}) async-start(), calls=%async_computation | async-start | bytes 8650752 | tf_op jit(solution)/shard_map/all_gather | solution.py:69
  36.2 522.1 %all-gather.5.cloned.1.call-start = ((), (), s32[]{:S(2)}) async-start(), calls=%async_computation.1 | async-start | bytes 8650752 | tf_op jit(solution)/shard_map/all_gather | solution.py:70
  83.7 2.0 copy-start
  99.1 2.0 copy-start.1
  442.7 10.7 %copy-start.3 = (f32[64]{0:T(128)S(1)}, f32[64]{0:T(128)}, u32[]{:S(2)}) copy-start(f32[64]{0:T(128)} %param.5) | copy-start | bytes 772
  459.1 106.4 %copy-start.2 = (f32[64,2048]{1,0:T(8,128)S(1)}, f32[64,2048]{1,0:T(8,128)}, u32[]{:S(2)}) copy-start(f32[64,2048]{1,0:T(8,128)} %param.3) | copy-start | bytes 1572868
Sparse Core Ops, SparseCore 0:
  36.4 101.4 all-gather.2
  451.8 106.4 all-gather.4
where the time goes:
time: 581 us; the launch traced here: 574 us
  other arithmetic  269 us (46%)
  waiting for transfers between devices  99.2 us (17%)
  matrix products  80.8 us (14%)
  blocking collectives  66.1 us (11%)
  local copies, waits for them, and re-layouts  38.5 us (7%)
  between operations  20.1 us (3%)
    another operation x30, other arithmetic, body(): diag_full = jnp.linalg.cholesky(diag_block)  172 us
    all_gather x1, waiting for transfers between devices, body(): lax.all_gather(panel_tile, 'col', axis=0, tiled=True)  99.2 us
    another operation x3, other arithmetic, body(): lax.linalg.triangular_solve(diag_full, identity, left_side=True, lower=True)  85.4 us
    all_gather x1, blocking collectives, body(): all_panel = lax.all_gather(panel_points, 'col', axis=1, tiled=True)  42.3 us
    another operation x15, matrix products, body(): lax.linalg.triangular_solve(diag_full, identity, left_side=True, lower=True)  28.1 us
    psum x1, blocking collectives, spread(): return lax.psum(block, axis)  23.8 us
    another operation x14, matrix products, body(): diag_full = jnp.linalg.cholesky(diag_block)  23.2 us
    another operation x24, local copies, waits for them, and re-layouts  23 us
  transfers between devices with their start and end apart: 2, of which 1 were waited for; matrix products, arithmetic and copies ran while one was open for 63% of the time, Pallas kernels for 0%

commit v1 on v0

v1 whole, which is shorter than its diff:
```python
import functools

import jax
import jax.numpy as jnp
from jax import lax
from jax.experimental import pallas as pl
from jax.experimental.pallas import tpu as pltpu
from jax.sharding import PartitionSpec as P

B = 1024
F = 64
RIDGE = 0.5
TILE = 128
REG = (8, 128)
NN = ((1,), (0,))
TN = ((0,), (0,))
NT = ((1,), (1,))


def mm(a, b, dims):
    return lax.dot_general(
        a, b, (dims, ((), ())), precision=lax.Precision.HIGHEST, preferred_element_type=jnp.float32
    )


def row_all(x, i):
    return jnp.broadcast_to(x[i : i + 1, :], REG)


def col_all(x, j):
    return jnp.broadcast_to(x[:, j : j + 1], REG)


def factor_tile(R):
    n = len(R)
    R = list(R)
    sub = lax.broadcasted_iota(jnp.int32, REG, 0)
    lane = lax.broadcasted_iota(jnp.int32, REG, 1)
    E = [jnp.where(lane == sub + 8 * q, 1.0, 0.0).astype(jnp.float32) for q in range(n)]
    U, G = [], []
    for p in range(n):
        C = {q: [col_all(R[q], 8 * p + k) for k in range(8)] for q in range(p, n)}
        d = [[row_all(C[p][k], i) if i >= k else None for k in range(8)] for i in range(8)]
        r = [row_all(R[p], i) for i in range(8)]
        e = [row_all(E[p], i) for i in range(8)]
        for s in range(8):
            rs = lax.rsqrt(d[s][s])
            l = {k: d[k][s] * rs for k in range(s + 1, 8)}
            for k in range(s + 1, 8):
                for m in range(s + 1, k + 1):
                    d[k][m] = d[k][m] - l[k] * l[m]
            r[s] = r[s] * rs
            e[s] = e[s] * rs
            for k in range(s + 1, 8):
                r[k] = r[k] - l[k] * r[s]
                e[k] = e[k] - l[k] * e[s]
            for q in range(p + 1, n):
                C[q][s] = C[q][s] * rs
                for k in range(s + 1, 8):
                    C[q][k] = C[q][k] - l[k] * C[q][s]
        for q in range(p + 1, n):
            for s in range(8):
                R[q] = R[q] - C[q][s] * r[s]
                E[q] = E[q] - C[q][s] * e[s]
        u, g = r[7], e[7]
        for s in range(6, -1, -1):
            u = jnp.where(sub == s, r[s], u)
            g = jnp.where(sub == s, e[s], g)
        U.append(u)
        G.append(g)
    return U, G


def unpack_points(packed):
    n = packed.shape[0] // 16
    halves = packed.reshape(n, 16, 2 * F)
    return jnp.concatenate([halves[:, :, :F], halves[:, :, F:]], axis=1).reshape(32 * n, F)


def factor_kernel(where_ref, pan_ref, look_ref, scales_ref, diag_ref, z_ref, a_ref, g_ref, b_ref):
    nb = B // TILE
    col, row = where_ref[0], where_ref[1]
    scales = scales_ref[...]
    points = unpack_points(pan_ref[...])
    weighted = points * scales
    look = unpack_points(look_ref[...])
    others = jnp.concatenate([points, look, jnp.zeros((TILE - look.shape[0], F), jnp.float32)], axis=0)
    ones = jnp.ones((8, F), jnp.float32)
    other_sq = mm(ones, others * others * scales, NT)[0:1, :]
    for i in range(nb):
        w = weighted[i * TILE : (i + 1) * TILE]
        sq = jnp.sum(w * points[i * TILE : (i + 1) * TILE], axis=1, keepdims=True)
        cross = mm(w, others, NT)
        block = jnp.exp(2.0 * cross - sq - other_sq)
        rid = lax.broadcasted_iota(jnp.int32, block.shape, 0) + i * TILE
        cid = lax.broadcasted_iota(jnp.int32, block.shape, 1)
        a_ref[i * TILE : (i + 1) * TILE, :] = jnp.where(rid == cid, block + RIDGE, block)

    width = 2 * TILE

    def step(k, carry):
        at = pl.multiple_of(k * TILE, TILE)
        here = pl.ds(at, TILE)
        big = k // 2
        R = [a_ref[pl.ds(at + 8 * q, 8), here] for q in range(TILE // 8)]
        U, G = factor_tile(R)
        g = jnp.concatenate(G, axis=0)
        g_ref[k] = g
        u = jnp.concatenate(U, axis=0)

        def panel(j, carry):
            cols = pl.ds(pl.multiple_of(j * width, width), width)
            a_ref[here, cols] = mm(g, a_ref[here, cols], NN)
            return carry

        lax.fori_loop(big, B // width, panel, 0)
        a_ref[here, B : B + TILE] = mm(g, a_ref[here, B : B + TILE], NN)
        a_ref[here, here] = u

        @pl.when(k % 2 == 0)
        def _():
            after = pl.ds(pl.multiple_of(at + TILE, TILE), TILE)
            side = a_ref[here, after]

            def update(j, carry):
                cols = pl.ds(pl.multiple_of(j * width, width), width)
                a_ref[after, cols] = a_ref[after, cols] - mm(side, a_ref[here, cols], TN)
                return carry

            lax.fori_loop(big, B // width, update, 0)
            a_ref[after, B : B + TILE] = a_ref[after, B : B + TILE] - mm(side, a_ref[here, B : B + TILE], TN)

        @pl.when(k % 2 == 1)
        def _():
            rows = pl.ds(pl.multiple_of(big * width, width), width)

            def update_rows(i, carry):
                dest = pl.ds(pl.multiple_of(i * width, width), width)
                side = a_ref[rows, dest]

                def update(j, carry):
                    cols = pl.ds(pl.multiple_of(j * width, width), width)
                    a_ref[dest, cols] = a_ref[dest, cols] - mm(side, a_ref[rows, cols], TN)
                    return carry

                lax.fori_loop(i, B // width, update, 0)
                a_ref[dest, B : B + TILE] = a_ref[dest, B : B + TILE] - mm(side, a_ref[rows, B : B + TILE], TN)
                return carry

            lax.fori_loop(big + 1, B // width, update_rows, 0)

        return carry

    lax.fori_loop(0, nb, step, 0)

    share = 32
    for k in range(nb):
        cols = slice(k * TILE, (k + 1) * TILE)
        r = lax.broadcasted_iota(jnp.int32, (share, TILE), 0) + col * share
        c = lax.broadcasted_iota(jnp.int32, (share, TILE), 1) + k * TILE
        b_ref[0:share, cols] = jnp.where(r == c, 1.0, 0.0).astype(jnp.float32)
        b_ref[share : 2 * share, cols] = a_ref[cols, B : B + TILE].T[0:share, :]
    for k in range(nb - 1, -1, -1):
        cols = slice(k * TILE, (k + 1) * TILE)
        z = mm(b_ref[:, cols], g_ref[k], NN)
        z_ref[:, cols] = z
        if k > 0:
            b_ref[:, 0 : k * TILE] = b_ref[:, 0 : k * TILE] - mm(z, a_ref[0 : k * TILE, cols], NT)

    own = pl.ds(pl.multiple_of(col * share, share), share)
    to = pl.multiple_of(row * TILE, TILE)
    tile = a_ref[own, pl.ds(to, TILE)]
    r = lax.broadcasted_iota(jnp.int32, (share, TILE), 0) + col * share
    c = lax.broadcasted_iota(jnp.int32, (share, TILE), 1) + to
    diag_ref[...] = jnp.where(c >= r, tile, 0.0).T


def rows_kernel(z_ref, pan_ref, look_ref, scales_ref, rows_ref, weight_ref, panel_ref, update_ref):
    scales = scales_ref[...]
    points = unpack_points(pan_ref[...])
    weighted = points * scales
    look = unpack_points(look_ref[...])
    look_weighted = look * scales
    rows = rows_ref[...]
    row_sq = jnp.sum(rows * rows * weight_ref[...], axis=0, keepdims=True)
    sq = jnp.sum(weighted * points, axis=1, keepdims=True)
    look_sq = jnp.sum(look_weighted * look, axis=1, keepdims=True)
    kernel = jnp.exp(2.0 * mm(weighted, rows, NN) - sq - row_sq)
    both = mm(z_ref[...], kernel, NN)
    look_rows = jnp.exp(2.0 * mm(look_weighted, rows, NN) - look_sq - row_sq)
    panel_ref[...] = both[0:32]
    update_ref[...] = look_rows - both[32:64]


def pack(points):
    rows = points.T
    return jnp.concatenate([rows[0:16], rows[16:32]], axis=1)


def local(where, panel, look, scales, row_points):
    share = 2 * look.shape[0]
    rows_dev = row_points.shape[1]
    scales_row = scales.reshape(1, F)
    scales_col = jnp.broadcast_to(scales.reshape(F, 1), (F, 128))[:, :1]
    vmem = pl.BlockSpec(memory_space=pltpu.VMEM)
    diag, z = pl.pallas_call(
        factor_kernel,
        out_shape=(
            jax.ShapeDtypeStruct((B // 8, share), jnp.float32),
            jax.ShapeDtypeStruct((2 * share, B), jnp.float32),
        ),
        in_specs=[pl.BlockSpec(memory_space=pltpu.SMEM), vmem, vmem, vmem],
        out_specs=(vmem, vmem),
        scratch_shapes=[
            pltpu.VMEM((B, B + TILE), jnp.float32),
            pltpu.VMEM((B // TILE, TILE, TILE), jnp.float32),
            pltpu.VMEM((2 * share, B), jnp.float32),
        ],
        name="factor",
    )(where, panel, look, scales_row)
    tile = 256
    fixed = lambda shape: pl.BlockSpec(shape, lambda j: (0, 0))
    cols = lambda n: pl.BlockSpec((n, tile), lambda j: (0, j))
    panel_tile, updated = pl.pallas_call(
        rows_kernel,
        grid=(rows_dev // tile,),
        out_shape=(
            jax.ShapeDtypeStruct((share, rows_dev), jnp.float32),
            jax.ShapeDtypeStruct((share, rows_dev), jnp.float32),
        ),
        in_specs=[fixed((2 * share, B)), fixed((B // 2, 2 * F)), fixed((share // 2, 2 * F)), fixed((1, F)), cols(F), fixed((F, 1))],
        out_specs=(cols(share), cols(share)),
        name="rows",
    )(z, panel, look, scales_row, row_points, scales_col)
    return (diag, panel_tile, updated)


def body(row_points, panel_points, scales):
    n_col = lax.axis_size("col")
    n_row = lax.axis_size("row")
    col = lax.axis_index("col")
    row = lax.axis_index("row")
    share = B // n_col
    rows_dev = row_points.shape[1]
    first = col * share
    look = pack(lax.dynamic_slice_in_dim(row_points, first % rows_dev, share, 1))
    look_all = lax.all_to_all(jnp.broadcast_to(look, (n_row,) + look.shape), "row", 0, 0, tiled=True)
    look = lax.dynamic_index_in_dim(look_all, first // rows_dev, 0, keepdims=False)
    own = pack(panel_points)
    panel = lax.all_to_all(jnp.broadcast_to(own, (n_col,) + own.shape), "col", 0, 0, tiled=True)
    panel = panel.reshape(B // 2, 2 * F)
    where = jnp.stack([col, row]).astype(jnp.int32)
    return local(where, panel, look, scales, row_points)


def solution(mesh):
    return jax.shard_map(
        body,
        mesh=mesh,
        in_specs=(P(None, "row"), P(None, "col"), P()),
        out_specs=(P("row", "col"), P("col", "row"), P("col", "row")),
        check_vma=False,
    )
```

time: 581 us -> 125 us (0.22); the launches traced: 574 us -> 125 us
  other arithmetic: 269 us -> 0.8 us
  Pallas kernels: 0 us -> 86.2 us
  waiting for transfers between devices: 99.2 us -> 13.4 us
  matrix products: 80.8 us -> 0 us
  blocking collectives: 66.1 us -> 0 us
  local copies, waits for them, and re-layouts: 38.5 us -> 6.46 us
  between operations: 20.1 us -> 0.7 us
  starting transfers between devices: 0.08 us -> 17.1 us
    another operation x33 -> x1, other arithmetic: 257 us -> 0.65 us  [body(): where = jnp.stack([col, row]).astype(jnp.int32)]
    all_gather x2 -> x0, waiting for transfers between devices: 99.2 us -> none  [the longest x1 99.2 us: body(): lax.all_gather(panel_tile, 'col', axis=0, tiled=True)]
    pallas_call x0 -> x2, Pallas kernels: none -> 86.2 us  [the longest x1 65.8 us: local(): pl.pallas_call(factor_kernel, out_shape=(jax.ShapeDtypeStruct((B // 8, sh...]
    another operation x29 -> x0, matrix products: 51.3 us -> none  [the longest x15 28.1 us: body(): lax.linalg.triangular_solve(diag_full, identity, left_side=True, lower=True)]
    all_gather x1 -> x0, blocking collectives: 42.3 us -> none  [body(): all_panel = lax.all_gather(panel_points, 'col', axis=1, tiled=True)]
    dot_general x7 -> x0, matrix products: 29.5 us -> none  [the longest x2 14.2 us: times_left(): jnp.dot(matrix, pieces, precision=lax.Precision.HIGHEST, preferred_elemen...]
    another operation x35 -> x0, local copies, waits for them, and re-layouts: 26.6 us -> none
    psum x1 -> x0, blocking collectives: 23.8 us -> none  [spread(): return lax.psum(block, axis)]
  transfers between devices with their start and end apart: 2 -> 2, of which waited for: 1 -> 2; matrix products, arithmetic and copies ran while one was open for 63% -> 2% of each run, Pallas kernels for 0% -> 0%
where the time goes in v1:
time: 125 us
  Pallas kernels  86.2 us (69%)
  starting transfers between devices  17.1 us (14%)
  waiting for transfers between devices  13.4 us (11%)
  local copies, waits for them, and re-layouts  6.46 us (5%)
    pallas_call x1, Pallas kernels, local(): pl.pallas_call(factor_kernel, out_shape=(jax.ShapeDtypeStruct((B // 8, sh...  65.8 us
    pallas_call x1, Pallas kernels, local(): pl.pallas_call(rows_kernel, grid=(rows_dev // tile,), out_shape=(jax.Shap...  20.4 us
    all_to_all x1, starting transfers between devices, body(): lax.all_to_all(jnp.broadcast_to(own, (n_col,) + own.shape), 'col', 0, 0,...  10.5 us
    all_to_all x1, waiting for transfers between devices, body(): lax.all_to_all(jnp.broadcast_to(own, (n_col,) + own.shape), 'col', 0, 0,...  8.59 us
    all_to_all x1, starting transfers between devices, body(): lax.all_to_all(jnp.broadcast_to(look, (n_row,) + look.shape), 'row', 0, 0...  6.63 us
    all_to_all x1, waiting for transfers between devices, body(): lax.all_to_all(jnp.broadcast_to(look, (n_row,) + look.shape), 'row', 0, 0...  4.79 us
    unnamed x8, local copies, waits for them, and re-layouts  2.95 us
  transfers between devices with their start and end apart: 2, of which 2 were waited for; matrix products, arithmetic and copies ran while one was open for 2% of the time, Pallas kernels for 0%

profile of v1, /device:TPU:1, one launch (start us, length us, event | category | flops | bytes accessed | tf_op | source)
XLA Modules:
  0.0 124.7 jit_solution(6966113158713799148)
XLA Ops:
  0.6 0.8 constant_dynamic-slice_fusion
  1.5 0.1 copy.12
  1.6 0.1 pad_maximum_fusion.1
  1.6 0.7 broadcast_in_dim.10
  2.3 0.0 copy-start.1
  2.3 6.6 %all-to-all-start.1 = ((f32[8,16,128]{2,1,0:T(8,128)}), f32[8,16,128]{2,1,0:T(8,128)S(1)}, u32[]{:S(2)}, u32[]{:S(2)}) async-start(f32[8,16,128]{2,1,0:T(8,128)} %broadcast_in_dim.10), calls=%async_computation.1 | async-start | bytes 131072 | tf_op jit(solution)/shard_map/all_to_all | solution.py:247
  8.9 0.0 copy-done.1
  8.9 0.1 pad_maximum_fusion
  9.0 4.8 %all-to-all-done.1 = f32[8,16,128]{2,1,0:T(8,128)S(1)} async-done(((f32[8,16,128]{2,1,0:T(8,128)}), f32[8,16,128]{2,1,0:T(8,128)S(1)}, u32[]{:S(2)}, u32[]{:S(2)}) %all-to-all-start.1) | async-done | bytes 65568 | tf_op jit(solution)/shard_map/all_to_all | solution.py:247
  13.8 0.7 broadcast_in_dim.4
  14.5 10.5 %all-to-all-start = ((f32[32,16,128]{2,1,0:T(8,128)}), f32[32,16,128]{2,1,0:T(8,128)S(1)}, u32[]{:S(2)}, u32[]{:S(2)}) async-start(f32[32,16,128]{2,1,0:T(8,128)} %broadcast_in_dim.4), calls=%async_computation | async-start | bytes 524288 | tf_op jit(solution)/shard_map/all_to_all | solution.py:250
  25.0 0.0 copy-start.2
  25.0 0.6 copy-done.2
  25.7 0.7 copy.10.weight_ref
  26.4 0.6 pad_add_fusion.where_ref
  27.0 0.6 dynamic-slice_bitcast_fusion.look_ref
  27.6 8.6 %all-to-all-done = f32[32,16,128]{2,1,0:T(8,128)S(1)} async-done(((f32[32,16,128]{2,1,0:T(8,128)}), f32[32,16,128]{2,1,0:T(8,128)S(1)}, u32[]{:S(2)}, u32[]{:S(2)}) %all-to-all-start) | async-done | bytes 262176 | tf_op jit(solution)/shard_map/all_to_all | solution.py:250
  36.2 0.0 copy-start
  36.2 0.7 copy-done
  36.9 65.8 %factor.1 = (f32[128,32]{1,0:T(8,128)}, f32[64,1024]{1,0:T(8,128)}) custom-call(s32[2]{0:T(128)} %pad_add_fusion.where_ref, f32[512,128]{1,0:T(8,128)} %bitcast.9, f32[16,128]{1,0:T(8,128)} %dynamic-slice_bitcast_fusion.look_ref, f32[1,64]{1,0:T(1,128)} %bitcast.13), custom_call_target="tpu_custom_call" | custom-call | tf_op jit(solution)/shard_map/factor/pallas_call | solution.py:206
  102.7 1.5 %copy.11 = f32[128,32]{0,1:T(8,128)} copy(f32[128,32]{1,0:T(8,128)} %get-tuple-element.14) | data formatting | bytes 32768
  104.3 20.4 %rows.1 = (f32[32,2048]{1,0:T(8,128)}, f32[32,2048]{1,0:T(8,128)}) custom-call(f32[64,1024]{1,0:T(8,128)} %get-tuple-element.8.z_ref, f32[512,128]{1,0:T(8,128)} %bitcast.10, f32[16,128]{1,0:T(8,128)} %dynamic-slice_bitcast_fusion.look_ref, f32[1,64]{1,0:T(1,128)} %bitcast.14, f32[64,2048]{1,0:T(8,128)} %rows_ref.1, f32[64,1]{1,0:T(8,128)} %copy.10.weight_ref), custom_call_target="tpu_custom_call" | custom-call | tf_op jit(solution)/shard_map/rows/pallas_call | solution.py:224
  (2 shorter events, 0.0 us)
Async XLA Ops:
  2.3 6.6 %copy-start.1 = (f32[64,32]{0,1:T(8,128)S(1)}, f32[64,32]{0,1:T(8,128)}, u32[]{:S(2)}) copy-start(f32[64,32]{0,1:T(8,128)} %param.4) | copy-start | bytes 24580
  2.3 11.5 %all-to-all-start.1 = ((f32[8,16,128]{2,1,0:T(8,128)}), f32[8,16,128]{2,1,0:T(8,128)S(1)}, u32[]{:S(2)}, u32[]{:S(2)}) async-start(f32[8,16,128]{2,1,0:T(8,128)} %broadcast_in_dim.10), calls=%async_computation.1 | async-start | bytes 131072 | tf_op jit(solution)/shard_map/all_to_all | solution.py:247
  14.5 21.7 %all-to-all-start = ((f32[32,16,128]{2,1,0:T(8,128)}), f32[32,16,128]{2,1,0:T(8,128)S(1)}, u32[]{:S(2)}, u32[]{:S(2)}) async-start(f32[32,16,128]{2,1,0:T(8,128)} %broadcast_in_dim.4), calls=%async_computation | async-start | bytes 524288 | tf_op jit(solution)/shard_map/all_to_all | solution.py:250
  25.0 0.7 copy-start.2
  36.2 0.7 copy-start

commit v2 on v1

v2 whole, which is shorter than its diff:
```python
import functools

import jax
import jax.numpy as jnp
from jax import lax
from jax.experimental import pallas as pl
from jax.experimental.pallas import tpu as pltpu
from jax.sharding import PartitionSpec as P

B = 1024
F = 64
RIDGE = 0.5
TILE = 128
REG = (8, 128)
NN = ((1,), (0,))
TN = ((0,), (0,))
NT = ((1,), (1,))


def mm(a, b, dims):
    return lax.dot_general(
        a, b, (dims, ((), ())), precision=lax.Precision.HIGHEST, preferred_element_type=jnp.float32
    )


def row_all(x, i):
    return jnp.broadcast_to(x[i : i + 1, :], REG)


def col_all(x, j):
    return jnp.broadcast_to(x[:, j : j + 1], REG)


def tree_sum(xs):
    xs=list(xs)
    while len(xs)>1:
        xs=[xs[i]+xs[i+1] if i+1<len(xs) else xs[i] for i in range(0,len(xs),2)]
    return xs[0]

def small_chol(d):
    d=[list(x) for x in d]
    rs=[None]*8; l=[[None]*8 for _ in range(8)]
    for s in range(8):
        rs[s]=lax.rsqrt(d[s][s])
        for k in range(s+1,8): l[k][s]=d[k][s]*rs[s]
        for k in range(s+1,8):
            for m in range(s+1,k+1):
                d[k][m]=d[k][m]-l[k][s]*l[m][s]
    return rs,l
def forward(x,rs,l):
    x=list(x)
    for s in range(8):
        x[s]=x[s]*rs[s]
        for k in range(s+1,8): x[k]=x[k]-l[k][s]*x[s]
    return x
def backward(x,rs,l):
    x=list(x)
    for s in range(7,-1,-1):
        x[s]=x[s]*rs[s]
        for k in range(s): x[k]=x[k]-l[s][k]*x[s]
    return x

def factor_tile(W, zero):
    n=len(W); W=list(W)
    sub=lax.broadcasted_iota(jnp.int32,REG,0); lane=lax.broadcasted_iota(jnp.int32,REG,1)
    G=[None]*n
    def entries(cols): return [[row_all(cols[k],i) if i>=k else None for k in range(8)] for i in range(8)]
    def finish(p, rs, l):
        mine=lax.shift_right_logical(lane,3)==p
        w=jnp.where(mine, jnp.where(lane-8*p==sub,1.0,0.0).astype(jnp.float32), W[p])
        w=forward([row_all(w,s) for s in range(8)],rs,l)
        g=w[7]
        for s in range(6,-1,-1): g=jnp.where(sub==s,w[s],g)
        G[p]=jnp.where(lane<8*(p+1),g,0.0)
        return mine,w
    for t in range(n//2):
        p0,p1=2*t,2*t+1
        c0={q:[col_all(W[q],8*p0+k) for k in range(8)] for q in range(p0,n)}
        d1=[col_all(W[p1],8*p1+k) for k in range(8)]
        rs,l=small_chol(entries([x+zero for x in c0[p0]]))
        x=forward(c0[p1],rs,l)
        d1=[d1[k]-tree_sum([x[s]*row_all(x[s],k) for s in range(8)]) for k in range(8)]
        mine,w=finish(p0,rs,l)
        W[p1]=jnp.where(mine,0.0,W[p1])-tree_sum([x[s]*w[s] for s in range(8)])
        v=backward(w,rs,l)
        for q in range(p1+1,n):
            W[q]=jnp.where(mine,0.0,W[q])-tree_sum([c0[q][s]*v[s] for s in range(8)])
        rs,l=small_chol(entries(d1))
        c1={q:[col_all(W[q],8*p1+k) for k in range(8)] for q in range(p1+1,n)}
        mine,w=finish(p1,rs,l)
        v=backward(w,rs,l)
        for q in range(p1+1,n):
            W[q]=jnp.where(mine,0.0,W[q])-tree_sum([c1[q][s]*v[s] for s in range(8)])
    return G

def unpack_points(packed):
    n = packed.shape[0] // 16
    halves = packed.reshape(n, 16, 2 * F)
    return jnp.concatenate([halves[:, :, :F], halves[:, :, F:]], axis=1).reshape(32 * n, F)


def split(x):
    high = x.astype(jnp.bfloat16)
    rest = x - high.astype(jnp.float32)
    middle = rest.astype(jnp.bfloat16)
    low = (rest - middle.astype(jnp.float32)).astype(jnp.bfloat16)
    return high, middle, low


def spread_terms(parts, order, values, axis):
    shape = list(parts[0].shape)
    shape[axis] = TILE
    place = lax.broadcasted_iota(jnp.int32, shape, axis)
    tail = jnp.zeros(shape, jnp.float32)
    for i, v in enumerate(values):
        tail = jnp.where(place == i, v, tail)
    return jnp.concatenate([parts[i] for i in order] + [tail.astype(jnp.bfloat16)], axis=axis)


def as_float(parts):
    return [p.astype(jnp.float32) for p in parts]


LEFT = (0, 0, 1, 0, 1, 2)
RIGHT = (0, 1, 0, 2, 1, 0)


def left_terms(points, scales):
    weighted = points * scales
    sq = jnp.sum(weighted * points, axis=1, keepdims=True)
    return spread_terms(split(2.0 * weighted), LEFT, as_float(split(-sq)) + [1.0, 1.0, 1.0], 1)


def right_terms(points, sq, axis):
    return spread_terms(split(points), RIGHT, [1.0, 1.0, 1.0] + as_float(split(-sq)), axis)


def dot16(a, b, dims):
    return lax.dot_general(a, b, (dims, ((), ())), preferred_element_type=jnp.float32)


def factor_kernel(where_ref, pan_ref, look_ref, scales_ref, zero_ref, diag_ref, z_ref, left_ref, a_ref, g_ref, b_ref, right_ref):
    nb = B // TILE
    col, row = where_ref[0], where_ref[1]
    scales = scales_ref[...]
    points = unpack_points(pan_ref[...])
    look = unpack_points(look_ref[...])
    share = look.shape[0]
    left_ref[0:B] = left_terms(points, scales)
    left_ref[B : B + share] = left_terms(look, scales)
    others = jnp.concatenate([points, look, jnp.zeros((TILE - share, F), jnp.float32)], axis=0)
    right_ref[...] = right_terms(others, jnp.sum(others * others * scales, axis=1, keepdims=True), 1)
    for i in range(nb):
        at = slice(i * TILE, (i + 1) * TILE)
        block = jnp.exp(dot16(left_ref[at], right_ref[i * TILE :], NT))
        a_ref[at, i * TILE :] = block
        rid = lax.broadcasted_iota(jnp.int32, (TILE, TILE), 0)
        cid = lax.broadcasted_iota(jnp.int32, (TILE, TILE), 1)
        a_ref[at, at] = jnp.where(rid == cid, block[:, 0:TILE] + RIDGE, block[:, 0:TILE])
        if i % 2 == 1:
            a_ref[at, (i - 1) * TILE : i * TILE] = jnp.zeros((TILE, TILE), jnp.float32)

    width = 2 * TILE

    def step(k, carry):
        at = pl.multiple_of(k * TILE, TILE)
        here = pl.ds(at, TILE)
        big = k // 2
        G = factor_tile([a_ref[pl.ds(at + 8 * q, 8), here] for q in range(TILE // 8)], zero_ref[...])
        for q in range(TILE // 8):
            g_ref[k, 8 * q : 8 * q + 8, :] = G[q]
        g = g_ref[k]

        def panel(j, carry):
            cols = pl.ds(pl.multiple_of(j * width, width), width)
            a_ref[here, cols] = mm(g, a_ref[here, cols], NN)
            return carry

        lax.fori_loop(big, B // width, panel, 0)
        a_ref[here, B : B + TILE] = mm(g, a_ref[here, B : B + TILE], NN)

        @pl.when(k % 2 == 0)
        def _():
            after = pl.ds(pl.multiple_of(at + TILE, TILE), TILE)
            side = a_ref[here, after]

            def update(j, carry):
                cols = pl.ds(pl.multiple_of(j * width, width), width)
                a_ref[after, cols] = a_ref[after, cols] - mm(side, a_ref[here, cols], TN)
                return carry

            lax.fori_loop(big, B // width, update, 0)
            a_ref[after, B : B + TILE] = a_ref[after, B : B + TILE] - mm(side, a_ref[here, B : B + TILE], TN)

        @pl.when(k % 2 == 1)
        def _():
            rows = pl.ds(pl.multiple_of(big * width, width), width)

            def update_rows(i, carry):
                dest = pl.ds(pl.multiple_of(i * width, width), width)
                side = a_ref[rows, dest]

                def update(j, carry):
                    cols = pl.ds(pl.multiple_of(j * width, width), width)
                    a_ref[dest, cols] = a_ref[dest, cols] - mm(side, a_ref[rows, cols], TN)
                    return carry

                lax.fori_loop(i, B // width, update, 0)
                a_ref[dest, B : B + TILE] = a_ref[dest, B : B + TILE] - mm(side, a_ref[rows, B : B + TILE], TN)
                return carry

            lax.fori_loop(big + 1, B // width, update_rows, 0)

        return carry

    lax.fori_loop(0, nb, step, 0)

    for k in range(nb):
        cols = slice(k * TILE, (k + 1) * TILE)
        r = lax.broadcasted_iota(jnp.int32, (share, TILE), 0) + col * share
        c = lax.broadcasted_iota(jnp.int32, (share, TILE), 1) + k * TILE
        b_ref[0:share, cols] = jnp.where(r == c, 1.0, 0.0).astype(jnp.float32)
        b_ref[share : 2 * share, cols] = a_ref[cols, B : B + TILE].T[0:share, :]
    for k in range(nb - 1, -1, -1):
        cols = slice(k * TILE, (k + 1) * TILE)
        z = mm(b_ref[:, cols], g_ref[k], NN)
        z_ref[:, cols] = z
        if k > 0:
            b_ref[:, 0 : k * TILE] = b_ref[:, 0 : k * TILE] - mm(z, a_ref[0 : k * TILE, cols], NT)

    own = pl.ds(pl.multiple_of(col * share, share), share)
    to = pl.multiple_of(row * TILE, TILE)
    tile = a_ref[own, pl.ds(to, TILE)]
    r = lax.broadcasted_iota(jnp.int32, (share, TILE), 0) + col * share
    c = lax.broadcasted_iota(jnp.int32, (share, TILE), 1) + to
    diag_ref[...] = jnp.where(c >= r, tile, 0.0).T


def rows_kernel(z_ref, left_ref, rows_ref, weight_ref, panel_ref, update_ref):
    share = panel_ref.shape[0]
    rows = rows_ref[...]
    sq = jnp.sum(rows * rows * weight_ref[...], axis=0, keepdims=True)
    kernel = jnp.exp(dot16(left_ref[...], right_terms(rows, sq, 0), NN))
    both = mm(z_ref[...], kernel[0:B], NN)
    panel_ref[...] = both[0:share]
    update_ref[...] = kernel[B : B + share] - both[share : 2 * share]


def pack(points):
    rows = points.T
    return jnp.concatenate([rows[0:16], rows[16:32]], axis=1)


def local(where, panel, look, scales, row_points):
    share = 2 * look.shape[0]
    rows_dev = row_points.shape[1]
    scales_row = scales.reshape(1, F)
    scales_col = scales.reshape(F, 1)
    vmem = pl.BlockSpec(memory_space=pltpu.VMEM)
    diag, z, left = pl.pallas_call(
        factor_kernel,
        out_shape=(
            jax.ShapeDtypeStruct((B // 8, share), jnp.float32),
            jax.ShapeDtypeStruct((2 * share, B), jnp.float32),
            jax.ShapeDtypeStruct((B + share, 4 * TILE), jnp.bfloat16),
        ),
        in_specs=[pl.BlockSpec(memory_space=pltpu.SMEM), vmem, vmem, vmem, vmem],
        out_specs=(vmem, vmem, vmem),
        scratch_shapes=[
            pltpu.VMEM((B, B + TILE), jnp.float32),
            pltpu.VMEM((B // TILE, TILE, TILE), jnp.float32),
            pltpu.VMEM((2 * share, B), jnp.float32),
            pltpu.VMEM((B + TILE, 4 * TILE), jnp.bfloat16),
        ],
        name="factor",
    )(where, panel, look, scales_row, jnp.zeros(REG, jnp.float32))
    tile = 256
    fixed = lambda shape: pl.BlockSpec(shape, lambda j: (0, 0))
    cols = lambda n: pl.BlockSpec((n, tile), lambda j: (0, j))
    panel_tile, updated = pl.pallas_call(
        rows_kernel,
        grid=(rows_dev // tile,),
        out_shape=(
            jax.ShapeDtypeStruct((share, rows_dev), jnp.float32),
            jax.ShapeDtypeStruct((share, rows_dev), jnp.float32),
        ),
        in_specs=[fixed((2 * share, B)), fixed((B + share, 4 * TILE)), cols(F), fixed((F, 1))],
        out_specs=(cols(share), cols(share)),
        name="rows",
    )(z, left, row_points, scales_col)
    return (diag, panel_tile, updated)


def body(row_points, panel_points, scales):
    n_col = lax.axis_size("col")
    n_row = lax.axis_size("row")
    col = lax.axis_index("col")
    row = lax.axis_index("row")
    share = B // n_col
    rows_dev = row_points.shape[1]
    first = col * share
    look = pack(lax.dynamic_slice_in_dim(row_points, first % rows_dev, share, 1))
    look_all = lax.all_to_all(jnp.broadcast_to(look, (n_row,) + look.shape), "row", 0, 0, tiled=True)
    look = lax.dynamic_index_in_dim(look_all, first // rows_dev, 0, keepdims=False)
    own = pack(panel_points)
    panel = lax.all_to_all(jnp.broadcast_to(own, (n_col,) + own.shape), "col", 0, 0, tiled=True)
    panel = panel.reshape(B // 2, 2 * F)
    where = jnp.stack([col, row]).astype(jnp.int32)
    return local(where, panel, look, scales, row_points)


def solution(mesh):
    return jax.shard_map(
        body,
        mesh=mesh,
        in_specs=(P(None, "row"), P(None, "col"), P()),
        out_specs=(P("row", "col"), P("col", "row"), P("col", "row")),
        check_vma=False,
    )
```

time: 125 us -> 105 us (0.84)
  Pallas kernels: 86.2 us -> 65.7 us
    pallas_call x1, Pallas kernels: 65.8 us -> 52.7 us  [local(): pl.pallas_call(factor_kernel, out_shape=(jax.ShapeDtypeStruct((B // 8, sh...]
    pallas_call x1, Pallas kernels: 20.4 us -> 13 us  [local(): pl.pallas_call(rows_kernel, grid=(rows_dev // tile,), out_shape=(jax.Shap...]
    unnamed x8 -> x6, local copies, waits for them, and re-layouts: 2.95 us -> 1.68 us
  transfers between devices with their start and end apart: 2 -> 2, of which waited for: 2 -> 2; matrix products, arithmetic and copies ran while one was open for 2% -> 3% of each run, Pallas kernels for 0% -> 0%
where the time goes in v2:
time: 105 us; the launch traced here: 104 us
  Pallas kernels  65.7 us (63%)
  starting transfers between devices  17 us (16%)
  waiting for transfers between devices  13.4 us (13%)
  local copies, waits for them, and re-layouts  6.52 us (6%)
    pallas_call x1, Pallas kernels, local(): pl.pallas_call(factor_kernel, out_shape=(jax.ShapeDtypeStruct((B // 8, sh...  52.7 us
    pallas_call x1, Pallas kernels, local(): pl.pallas_call(rows_kernel, grid=(rows_dev // tile,), out_shape=(jax.Shap...  13 us
    all_to_all x1, starting transfers between devices, body(): lax.all_to_all(jnp.broadcast_to(own, (n_col,) + own.shape), 'col', 0, 0,...  10.5 us
    all_to_all x1, waiting for transfers between devices, body(): lax.all_to_all(jnp.broadcast_to(own, (n_col,) + own.shape), 'col', 0, 0,...  9.31 us
    all_to_all x1, starting transfers between devices, body(): lax.all_to_all(jnp.broadcast_to(look, (n_row,) + look.shape), 'row', 0, 0...  6.49 us
    all_to_all x1, waiting for transfers between devices, body(): lax.all_to_all(jnp.broadcast_to(look, (n_row,) + look.shape), 'row', 0, 0...  4.08 us
  transfers between devices with their start and end apart: 2, of which 2 were waited for; matrix products, arithmetic and copies ran while one was open for 3% of the time, Pallas kernels for 0%

profile of v2, /device:TPU:1, one launch (start us, length us, event | category | flops | bytes accessed | tf_op | source)
XLA Modules:
  0.0 104.0 jit_solution(13473447852399071396)
XLA Ops:
  0.6 0.0 copy-start.1
  0.7 0.8 constant_dynamic-slice_fusion
  1.5 0.1 copy.12
  1.6 0.1 pad_maximum_fusion.1
  1.7 0.7 broadcast_in_dim.10
  2.3 6.5 %all-to-all-start.1 = ((f32[8,16,128]{2,1,0:T(8,128)}), f32[8,16,128]{2,1,0:T(8,128)S(1)}, u32[]{:S(2)}, u32[]{:S(2)}) async-start(f32[8,16,128]{2,1,0:T(8,128)} %broadcast_in_dim.10), calls=%async_computation.1 | async-start | bytes 131072 | tf_op jit(solution)/shard_map/all_to_all | solution.py:303
  8.8 0.7 fusion.1
  9.5 0.1 pad_maximum_fusion
  9.6 4.1 %all-to-all-done.1 = f32[8,16,128]{2,1,0:T(8,128)S(1)} async-done(((f32[8,16,128]{2,1,0:T(8,128)}), f32[8,16,128]{2,1,0:T(8,128)S(1)}, u32[]{:S(2)}, u32[]{:S(2)}) %all-to-all-start.1) | async-done | bytes 65568 | tf_op jit(solution)/shard_map/all_to_all | solution.py:303
  13.7 0.7 broadcast_in_dim.9
  14.4 10.5 %all-to-all-start = ((f32[32,16,128]{2,1,0:T(8,128)}), f32[32,16,128]{2,1,0:T(8,128)S(1)}, u32[]{:S(2)}, u32[]{:S(2)}) async-start(f32[32,16,128]{2,1,0:T(8,128)} %broadcast_in_dim.9), calls=%async_computation | async-start | bytes 524288 | tf_op jit(solution)/shard_map/all_to_all | solution.py:306
  24.9 0.0 copy-done.1
  24.9 0.7 copy.10.weight_ref
  25.6 0.6 pad_add_fusion.where_ref
  26.2 0.6 dynamic-slice_bitcast_fusion.look_ref
  26.8 9.3 %all-to-all-done = f32[32,16,128]{2,1,0:T(8,128)S(1)} async-done(((f32[32,16,128]{2,1,0:T(8,128)}), f32[32,16,128]{2,1,0:T(8,128)S(1)}, u32[]{:S(2)}, u32[]{:S(2)}) %all-to-all-start) | async-done | bytes 262176 | tf_op jit(solution)/shard_map/all_to_all | solution.py:306
  36.1 0.0 copy-start
  36.1 0.6 broadcast_in_dim.11.zero_ref
  36.7 0.1 copy-done
  36.8 52.7 %factor.1 = (f32[128,32]{1,0:T(8,128)}, f32[64,1024]{1,0:T(8,128)}, bf16[1056,512]{1,0:T(8,128)(2,1)}) custom-call(s32[2]{0:T(128)} %pad_add_fusion.where_ref, f32[512,128]{1,0:T(8,128)} %bitcast.9, f32[16,128]{1,0:T(8,128)} %dynamic-slice_bitcast_fusion.look_ref, f32[1,64]{1,0:T(1,128)} %bitcast.12, f32[8,128]{1,0:T(8,128)} %broadcast_in_dim.11.zero_ref), custom_call_target="tpu_custom_call" | custom-call | tf_op jit(solution)/shard_map/factor/pallas_call | solution.py:260
  89.5 1.5 %copy.11 = f32[128,32]{0,1:T(8,128)} copy(f32[128,32]{1,0:T(8,128)} %get-tuple-element.16) | data formatting | bytes 32768
  91.1 13.0 %rows.1 = (f32[32,2048]{1,0:T(8,128)}, f32[32,2048]{1,0:T(8,128)}) custom-call(f32[64,1024]{1,0:T(8,128)} %get-tuple-element.9.z_ref, bf16[1056,512]{1,0:T(8,128)(2,1)} %get-tuple-element.10.left_ref, f32[64,2048]{1,0:T(8,128)} %rows_ref.1, f32[64,1]{1,0:T(8,128)} %copy.10.weight_ref), custom_call_target="tpu_custom_call" | custom-call | tf_op jit(solution)/shard_map/rows/pallas_call | solution.py:280
  (1 shorter events, 0.0 us)
Async XLA Ops:
  0.6 24.3 %copy-start.1 = (f32[64]{0:T(128)S(1)}, f32[64]{0:T(128)}, u32[]{:S(2)}) copy-start(f32[64]{0:T(128)} %param.5) | copy-start | bytes 772
  2.3 11.4 %all-to-all-start.1 = ((f32[8,16,128]{2,1,0:T(8,128)}), f32[8,16,128]{2,1,0:T(8,128)S(1)}, u32[]{:S(2)}, u32[]{:S(2)}) async-start(f32[8,16,128]{2,1,0:T(8,128)} %broadcast_in_dim.10), calls=%async_computation.1 | async-start | bytes 131072 | tf_op jit(solution)/shard_map/all_to_all | solution.py:303
  14.4 21.7 %all-to-all-start = ((f32[32,16,128]{2,1,0:T(8,128)}), f32[32,16,128]{2,1,0:T(8,128)S(1)}, u32[]{:S(2)}, u32[]{:S(2)}) async-start(f32[32,16,128]{2,1,0:T(8,128)} %broadcast_in_dim.9), calls=%async_computation | async-start | bytes 524288 | tf_op jit(solution)/shard_map/all_to_all | solution.py:306
  36.1 0.7 copy-start

commit v3 on v2

--- a/solution.py
+++ b/solution.py
@@ -139,7 +139,11 @@
     return lax.dot_general(a, b, (dims, ((), ())), preferred_element_type=jnp.float32)
 
 
-def factor_kernel(where_ref, pan_ref, look_ref, scales_ref, zero_ref, diag_ref, z_ref, left_ref, a_ref, g_ref, b_ref, right_ref):
+def panel_kernel(
+    where_ref, pan_ref, look_ref, scales_ref, zero_ref, rows_ref, weight_ref,
+    diag_ref, panel_ref, update_ref,
+    z_ref, left_ref, a_ref, g_ref, b_ref, right_ref, kern_ref,
+):
     nb = B // TILE
     col, row = where_ref[0], where_ref[1]
     scales = scales_ref[...]
@@ -160,57 +164,30 @@
         if i % 2 == 1:
             a_ref[at, (i - 1) * TILE : i * TILE] = jnp.zeros((TILE, TILE), jnp.float32)
 
-    width = 2 * TILE
+    wide = rows_ref.shape[1] // nb
+
+    def after_tile(k):
+        here = slice(k * TILE, (k + 1) * TILE)
+        a_ref[here, k * TILE :] = mm(g_ref[k], a_ref[here, k * TILE :], NN)
+        if k % 2 == 0:
+            later = slice((k + 1) * TILE, (k + 2) * TILE)
+            a_ref[later, later.start :] -= mm(a_ref[here, later], a_ref[here, later.start :], TN)
+        else:
+            pair = slice((k - 1) * TILE, (k + 1) * TILE)
+            for i in range(k + 1, nb, 2):
+                later = slice(i * TILE, (i + 2) * TILE)
+                a_ref[later, i * TILE :] -= mm(a_ref[pair, later], a_ref[pair, i * TILE :], TN)
 
     def step(k, carry):
         at = pl.multiple_of(k * TILE, TILE)
-        here = pl.ds(at, TILE)
-        big = k // 2
-        G = factor_tile([a_ref[pl.ds(at + 8 * q, 8), here] for q in range(TILE // 8)], zero_ref[...])
+        G = factor_tile([a_ref[pl.ds(at + 8 * q, 8), pl.ds(at, TILE)] for q in range(TILE // 8)], zero_ref[...])
         for q in range(TILE // 8):
             g_ref[k, 8 * q : 8 * q + 8, :] = G[q]
-        g = g_ref[k]
-
-        def panel(j, carry):
-            cols = pl.ds(pl.multiple_of(j * width, width), width)
-            a_ref[here, cols] = mm(g, a_ref[here, cols], NN)
-            return carry
-
-        lax.fori_loop(big, B // width, panel, 0)
-        a_ref[here, B : B + TILE] = mm(g, a_ref[here, B : B + TILE], NN)
-
-        @pl.when(k % 2 == 0)
-        def _():
-            after = pl.ds(pl.multiple_of(at + TILE, TILE), TILE)
-            side = a_ref[here, after]
-
-            def update(j, carry):
-                cols = pl.ds(pl.multiple_of(j * width, width), width)
-                a_ref[after, cols] = a_ref[after, cols] - mm(side, a_ref[here, cols], TN)
-                return carry
-
-            lax.fori_loop(big, B // width, update, 0)
-            a_ref[after, B : B + TILE] = a_ref[after, B : B + TILE] - mm(side, a_ref[here, B : B + TILE], TN)
-
-        @pl.when(k % 2 == 1)
-        def _():
-            rows = pl.ds(pl.multiple_of(big * width, width), width)
-
-            def update_rows(i, carry):
-                dest = pl.ds(pl.multiple_of(i * width, width), width)
-                side = a_ref[rows, dest]
-
-                def update(j, carry):
-                    cols = pl.ds(pl.multiple_of(j * width, width), width)
-                    a_ref[dest, cols] = a_ref[dest, cols] - mm(side, a_ref[rows, cols], TN)
-                    return carry
-
-                lax.fori_loop(i, B // width, update, 0)
-                a_ref[dest, B : B + TILE] = a_ref[dest, B : B + TILE] - mm(side, a_ref[rows, B : B + TILE], TN)
-                return carry
-
-            lax.fori_loop(big + 1, B // width, update_rows, 0)
-
+        to = pl.ds(pl.multiple_of(k * wide, wide), wide)
+        rows = rows_ref[:, to]
+        sq = jnp.sum(rows * rows * weight_ref[...], axis=0, keepdims=True)
+        kern_ref[:, to] = jnp.exp(dot16(left_ref[...], right_terms(rows, sq, 0), NN))
+        lax.switch(k, [functools.partial(after_tile, i) for i in range(nb)])
         return carry
 
     lax.fori_loop(0, nb, step, 0)
@@ -233,17 +210,18 @@
     tile = a_ref[own, pl.ds(to, TILE)]
     r = lax.broadcasted_iota(jnp.int32, (share, TILE), 0) + col * share
     c = lax.broadcasted_iota(jnp.int32, (share, TILE), 1) + to
-    diag_ref[...] = jnp.where(c >= r, tile, 0.0).T
-
-
-def rows_kernel(z_ref, left_ref, rows_ref, weight_ref, panel_ref, update_ref):
-    share = panel_ref.shape[0]
-    rows = rows_ref[...]
-    sq = jnp.sum(rows * rows * weight_ref[...], axis=0, keepdims=True)
-    kernel = jnp.exp(dot16(left_ref[...], right_terms(rows, sq, 0), NN))
-    both = mm(z_ref[...], kernel[0:B], NN)
-    panel_ref[...] = both[0:share]
-    update_ref[...] = kernel[B : B + share] - both[share : 2 * share]
+    diag_ref[...] = jnp.where(c >= r, tile, 0.0)
+
+    block = 2 * wide
+
+    def product(j, carry):
+        to = pl.ds(pl.multiple_of(j * block, block), block)
+        both = mm(z_ref[...], kern_ref[0:B, to], NN)
+        panel_ref[:, to] = both[0:share]
+        update_ref[:, to] = kern_ref[B : B + share, to] - both[share : 2 * share]
+        return carry
+
+    lax.fori_loop(0, rows_ref.shape[1] // block, product, 0)
 
 
 def pack(points):
@@ -257,38 +235,24 @@
     scales_row = scales.reshape(1, F)
     scales_col = scales.reshape(F, 1)
     vmem = pl.BlockSpec(memory_space=pltpu.VMEM)
-    diag, z, left = pl.pallas_call(
-        factor_kernel,
-        out_shape=(
-            jax.ShapeDtypeStruct((B // 8, share), jnp.float32),
-            jax.ShapeDtypeStruct((2 * share, B), jnp.float32),
-            jax.ShapeDtypeStruct((B + share, 4 * TILE), jnp.bfloat16),
-        ),
-        in_specs=[pl.BlockSpec(memory_space=pltpu.SMEM), vmem, vmem, vmem, vmem],
+    out = jax.ShapeDtypeStruct((share, rows_dev), jnp.float32)
+    diag, panel_tile, updated = pl.pallas_call(
+        panel_kernel,
+        out_shape=(jax.ShapeDtypeStruct((share, B // 8), jnp.float32), out, out),
+        in_specs=[pl.BlockSpec(memory_space=pltpu.SMEM)] + [vmem] * 6,
         out_specs=(vmem, vmem, vmem),
         scratch_shapes=[
+            pltpu.VMEM((2 * share, B), jnp.float32),
+            pltpu.VMEM((B + share, 4 * TILE), jnp.bfloat16),
             pltpu.VMEM((B, B + TILE), jnp.float32),
             pltpu.VMEM((B // TILE, TILE, TILE), jnp.float32),
             pltpu.VMEM((2 * share, B), jnp.float32),
             pltpu.VMEM((B + TILE, 4 * TILE), jnp.bfloat16),
+            pltpu.VMEM((B + share, rows_dev), jnp.float32),
         ],
-        name="factor",
-    )(where, panel, look, scales_row, jnp.zeros(REG, jnp.float32))
-    tile = 256
-    fixed = lambda shape: pl.BlockSpec(shape, lambda j: (0, 0))
-    cols = lambda n: pl.BlockSpec((n, tile), lambda j: (0, j))
-    panel_tile, updated = pl.pallas_call(
-        rows_kernel,
-        grid=(rows_dev // tile,),
-        out_shape=(
-            jax.ShapeDtypeStruct((share, rows_dev), jnp.float32),
-            jax.ShapeDtypeStruct((share, rows_dev), jnp.float32),
-        ),
-        in_specs=[fixed((2 * share, B)), fixed((B + share, 4 * TILE)), cols(F), fixed((F, 1))],
-        out_specs=(cols(share), cols(share)),
-        name="rows",
-    )(z, left, row_points, scales_col)
-    return (diag, panel_tile, updated)
+        name="panel",
+    )(where, panel, look, scales_row, jnp.zeros(REG, jnp.float32), row_points, scales_col)
+    return (diag.T, panel_tile, updated)
 
 
 def body(row_points, panel_points, scales):
@@ -299,12 +263,12 @@
     share = B // n_col
     rows_dev = row_points.shape[1]
     first = col * share
-    look = pack(lax.dynamic_slice_in_dim(row_points, first % rows_dev, share, 1))
-    look_all = lax.all_to_all(jnp.broadcast_to(look, (n_row,) + look.shape), "row", 0, 0, tiled=True)
-    look = lax.dynamic_index_in_dim(look_all, first // rows_dev, 0, keepdims=False)
     own = pack(panel_points)
     panel = lax.all_to_all(jnp.broadcast_to(own, (n_col,) + own.shape), "col", 0, 0, tiled=True)
     panel = panel.reshape(B // 2, 2 * F)
+    look = pack(lax.dynamic_slice_in_dim(row_points, first % rows_dev, share, 1))
+    sent = [lax.ppermute(look, "row", [(0, to)]) for to in range(1, n_row)]
+    look = jnp.where(row == 0, look, sum(sent[1:], sent[0]))
     where = jnp.stack([col, row]).astype(jnp.int32)
     return local(where, panel, look, scales, row_points)
 

time: 105 us -> 80.2 us (0.76)
  Pallas kernels: 65.7 us -> 49.5 us
  waiting for transfers between devices: 13.4 us -> 6.36 us
  local copies, waits for them, and re-layouts: 6.52 us -> 4.39 us
    pallas_call x2 -> x1, Pallas kernels: 65.7 us -> 49.5 us  [local(): pl.pallas_call(panel_kernel, out_shape=(jax.ShapeDtypeStruct((share, B //...]
    all_to_all x1, waiting for transfers between devices: 9.31 us -> 0.01 us  [body(): lax.all_to_all(jnp.broadcast_to(own, (n_col,) + own.shape), 'col', 0, 0,...]
    all_to_all x1 -> x0, starting transfers between devices: 6.49 us -> none  [body(): lax.all_to_all(jnp.broadcast_to(look, (n_row,) + look.shape), 'row', 0, 0...]
    ppermute x0 -> x7, waiting for transfers between devices: none -> 6.35 us  [body(): sent = [lax.ppermute(look, 'row', [(0, to)]) for to in range(1, n_row)]]
    ppermute x0 -> x7, starting transfers between devices: none -> 5.26 us  [body(): sent = [lax.ppermute(look, 'row', [(0, to)]) for to in range(1, n_row)]]
    all_to_all x1 -> x0, waiting for transfers between devices: 4.08 us -> none  [body(): lax.all_to_all(jnp.broadcast_to(look, (n_row,) + look.shape), 'row', 0, 0...]
    all_to_all x1, starting transfers between devices: 10.5 us -> 11.9 us  [body(): lax.all_to_all(jnp.broadcast_to(own, (n_col,) + own.shape), 'col', 0, 0,...]
  transfers between devices with their start and end apart: 2 -> 8, of which waited for: 2 -> 1; matrix products, arithmetic and copies ran while one was open for 3% -> 4% of each run, Pallas kernels for 0% -> 0%
where the time goes in v3:
time: 80.2 us; the launch traced here: 79.5 us
  Pallas kernels  49.5 us (62%)
  starting transfers between devices  17.1 us (21%)
  waiting for transfers between devices  6.36 us (8%)
  local copies, waits for them, and re-layouts  4.39 us (5%)
  other arithmetic  1.42 us (2%)
    pallas_call x1, Pallas kernels, local(): pl.pallas_call(panel_kernel, out_shape=(jax.ShapeDtypeStruct((share, B //...  49.5 us
    all_to_all x1, starting transfers between devices, body(): lax.all_to_all(jnp.broadcast_to(own, (n_col,) + own.shape), 'col', 0, 0,...  11.9 us
    ppermute x7, waiting for transfers between devices, body(): sent = [lax.ppermute(look, 'row', [(0, to)]) for to in range(1, n_row)]  6.35 us
    ppermute x7, starting transfers between devices, body(): sent = [lax.ppermute(look, 'row', [(0, to)]) for to in range(1, n_row)]  5.26 us
  transfers between devices with their start and end apart: 8, of which 1 were waited for; matrix products, arithmetic and copies ran while one was open for 4% of the time, Pallas kernels for 0%

profile of v3, /device:TPU:1, one launch (start us, length us, event | category | flops | bytes accessed | tf_op | source)
XLA Modules:
  0.0 79.5 jit_solution(9122144416738604887)
XLA Ops:
  0.6 0.7 fusion.1
  1.3 0.1 pad_maximum_fusion
  1.4 0.7 broadcast_in_dim.6
  2.1 11.9 %all-to-all-start = ((f32[32,16,128]{2,1,0:T(8,128)}), f32[32,16,128]{2,1,0:T(8,128)S(1)}, u32[]{:S(2)}, u32[]{:S(2)}) async-start(f32[32,16,128]{2,1,0:T(8,128)} %broadcast_in_dim.6), calls=%async_computation | async-start | bytes 524288 | tf_op jit(solution)/shard_map/all_to_all | solution.py:267
  14.0 0.8 %constant_dynamic-slice_fusion = f32[64,32]{1,0:T(8,128)S(1)} fusion(f32[64,2048]{1,0:T(8,128)} %rows_ref.1, s32[]{:T(128)S(6)} %select_n.20), kind=kLoop, calls=%fused_computation.4 | loop fusion | bytes 16388 | tf_op jit(solution)/shard_map/dynamic_slice | solution.py:269
  14.9 0.1 copy.8
  14.9 0.1 pad_maximum_fusion.1
  15.0 0.7 collective-permute-start.6
  15.7 0.7 collective-permute-start.5
  16.4 0.7 collective-permute-start.4
  17.0 0.7 collective-permute-start.3
  17.7 0.7 collective-permute-start.2
  18.4 0.0 collective-permute-done.6
  18.4 0.7 collective-permute-start.1
  19.1 0.0 collective-permute-done.5
  19.1 1.3 %collective-permute-start = (f32[16,128]{1,0:T(8,128)S(1)}, f32[16,128]{1,0:T(8,128)S(1)}, u32[]{:S(2)}, u32[]{:S(2)}) collective-permute-start(f32[16,128]{1,0:T(8,128)S(1)} %pad_maximum_fusion.1), channel_id=1, source_target_pairs={{0,32},{1,33},{2,34},{3,35},{4,36},{5,37},{6,38},{7,39},{8,40},{9,... | collective-permute-start | bytes 24584 | tf_op jit(solution)/shard_map/ppermute | solution.py:270
  20.4 0.7 pad_add_fusion.where_ref
  21.0 0.0 copy-start.1
  21.0 0.7 copy-done.1
  21.7 0.7 copy.7.weight_ref
  22.4 0.0 collective-permute-done.4
  22.4 0.0 collective-permute-done.3
  22.4 0.0 collective-permute-done.2
  22.4 0.0 collective-permute-done.1
  22.4 6.3 %collective-permute-done = f32[16,128]{1,0:T(8,128)S(1)} collective-permute-done((f32[16,128]{1,0:T(8,128)S(1)}, f32[16,128]{1,0:T(8,128)S(1)}, u32[]{:S(2)}, u32[]{:S(2)}) %collective-permute-start) | collective-permute-done | bytes 8224 | tf_op jit(solution)/shard_map/ppermute | solution.py:270
  28.7 0.6 add_select_fusion.look_ref
  29.3 0.0 all-to-all-done
  29.3 0.0 copy-start
  29.3 0.6 broadcast_in_dim.7.zero_ref
  30.0 0.1 copy-done
  30.0 49.5 %panel.1 = (f32[32,128]{1,0:T(8,128)}, f32[32,2048]{1,0:T(8,128)}, f32[32,2048]{1,0:T(8,128)}) custom-call(s32[2]{0:T(128)} %pad_add_fusion.where_ref, f32[512,128]{1,0:T(8,128)} %bitcast.8, f32[16,128]{1,0:T(8,128)} %add_select_fusion.look_ref, f32[1,64]{1,0:T(1,128)} %bitcast.11, f32[8,128]{1,0:T(8,128)} %broadcast_in_dim.7.zero_ref, f32[64,2048]{1,0:T(8,128)} %rows_ref.1, ...), custom_call_target="tpu_custom_call" | custom-call | tf_op jit(solution)/shard_map/panel/pallas_call | solution.py:239
  (1 shorter events, 0.0 us)
Async XLA Ops:
  2.1 27.2 %all-to-all-start = ((f32[32,16,128]{2,1,0:T(8,128)}), f32[32,16,128]{2,1,0:T(8,128)S(1)}, u32[]{:S(2)}, u32[]{:S(2)}) async-start(f32[32,16,128]{2,1,0:T(8,128)} %broadcast_in_dim.6), calls=%async_computation | async-start | bytes 524288 | tf_op jit(solution)/shard_map/all_to_all | solution.py:267
  15.0 3.4 %collective-permute-start.6 = (f32[16,128]{1,0:T(8,128)S(1)}, f32[16,128]{1,0:T(8,128)S(1)}, u32[]{:S(2)}, u32[]{:S(2)}) collective-permute-start(f32[16,128]{1,0:T(8,128)S(1)} %pad_maximum_fusion.1), channel_id=1, source_target_pairs={{0,224},{1,225},{2,226},{3,227},{4,228},{5,229},{6,230},{7,231},{8... | collective-permute-start | bytes 24584 | tf_op jit(solution)/shard_map/ppermute | solution.py:270
  15.7 3.4 %collective-permute-start.5 = (f32[16,128]{1,0:T(8,128)S(1)}, f32[16,128]{1,0:T(8,128)S(1)}, u32[]{:S(2)}, u32[]{:S(2)}) collective-permute-start(f32[16,128]{1,0:T(8,128)S(1)} %pad_maximum_fusion.1), channel_id=1, source_target_pairs={{0,192},{1,193},{2,194},{3,195},{4,196},{5,197},{6,198},{7,199},{8... | collective-permute-start | bytes 24584 | tf_op jit(solution)/shard_map/ppermute | solution.py:270
  16.4 6.0 %collective-permute-start.4 = (f32[16,128]{1,0:T(8,128)S(1)}, f32[16,128]{1,0:T(8,128)S(1)}, u32[]{:S(2)}, u32[]{:S(2)}) collective-permute-start(f32[16,128]{1,0:T(8,128)S(1)} %pad_maximum_fusion.1), channel_id=1, source_target_pairs={{0,160},{1,161},{2,162},{3,163},{4,164},{5,165},{6,166},{7,167},{8... | collective-permute-start | bytes 24584 | tf_op jit(solution)/shard_map/ppermute | solution.py:270
  17.0 5.3 %collective-permute-start.3 = (f32[16,128]{1,0:T(8,128)S(1)}, f32[16,128]{1,0:T(8,128)S(1)}, u32[]{:S(2)}, u32[]{:S(2)}) collective-permute-start(f32[16,128]{1,0:T(8,128)S(1)} %pad_maximum_fusion.1), channel_id=1, source_target_pairs={{0,128},{1,129},{2,130},{3,131},{4,132},{5,133},{6,134},{7,135},{8... | collective-permute-start | bytes 24584 | tf_op jit(solution)/shard_map/ppermute | solution.py:270
  17.7 4.7 %collective-permute-start.2 = (f32[16,128]{1,0:T(8,128)S(1)}, f32[16,128]{1,0:T(8,128)S(1)}, u32[]{:S(2)}, u32[]{:S(2)}) collective-permute-start(f32[16,128]{1,0:T(8,128)S(1)} %pad_maximum_fusion.1), channel_id=1, source_target_pairs={{0,96},{1,97},{2,98},{3,99},{4,100},{5,101},{6,102},{7,103},{8,104... | collective-permute-start | bytes 24584 | tf_op jit(solution)/shard_map/ppermute | solution.py:270
  18.4 4.0 %collective-permute-start.1 = (f32[16,128]{1,0:T(8,128)S(1)}, f32[16,128]{1,0:T(8,128)S(1)}, u32[]{:S(2)}, u32[]{:S(2)}) collective-permute-start(f32[16,128]{1,0:T(8,128)S(1)} %pad_maximum_fusion.1), channel_id=1, source_target_pairs={{0,64},{1,65},{2,66},{3,67},{4,68},{5,69},{6,70},{7,71},{8,72},{9,... | collective-permute-start | bytes 24584 | tf_op jit(solution)/shard_map/ppermute | solution.py:270
  19.1 9.7 %collective-permute-start = (f32[16,128]{1,0:T(8,128)S(1)}, f32[16,128]{1,0:T(8,128)S(1)}, u32[]{:S(2)}, u32[]{:S(2)}) collective-permute-start(f32[16,128]{1,0:T(8,128)S(1)} %pad_maximum_fusion.1), channel_id=1, source_target_pairs={{0,32},{1,33},{2,34},{3,35},{4,36},{5,37},{6,38},{7,39},{8,40},{9,... | collective-permute-start | bytes 24584 | tf_op jit(solution)/shard_map/ppermute | solution.py:270
  21.0 0.7 copy-start.1
  29.3 0.7 copy-start

commit v4 on v3

--- a/solution.py
+++ b/solution.py
@@ -12,6 +12,7 @@
 RIDGE = 0.5
 TILE = 128
 REG = (8, 128)
+NEAR = 4
 NN = ((1,), (0,))
 TN = ((0,), (0,))
 NT = ((1,), (1,))
@@ -40,12 +41,26 @@
 def small_chol(d):
     d=[list(x) for x in d]
     rs=[None]*8; l=[[None]*8 for _ in range(8)]
-    for s in range(8):
-        rs[s]=lax.rsqrt(d[s][s])
-        for k in range(s+1,8): l[k][s]=d[k][s]*rs[s]
-        for k in range(s+1,8):
-            for m in range(s+1,k+1):
-                d[k][m]=d[k][m]-l[k][s]*l[m][s]
+    for s in range(0,8,2):
+        a,b,c=d[s][s],d[s+1][s],d[s+1][s+1]
+        det=a*c-b*b
+        r0=lax.rsqrt(a)
+        l10=b*r0
+        rd=lax.rsqrt(det)
+        inv=rd*rd
+        r1=(a*r0)*rd
+        r01=r0*rd
+        rs[s]=r0; rs[s+1]=r1
+        l[s+1][s]=l10
+        y0={};y1={}
+        for k in range(s+2,8):
+            y0[k]=c*d[k][s]-b*d[k][s+1]
+            y1[k]=a*d[k][s+1]-b*d[k][s]
+            l[k][s]=d[k][s]*r0
+            l[k][s+1]=y1[k]*r01
+        for k in range(s+2,8):
+            for m in range(s+2,k+1):
+                d[k][m]=d[k][m]-(y0[k]*d[m][s]+y1[k]*d[m][s+1])*inv
     return rs,l
 def forward(x,rs,l):
     x=list(x)
@@ -75,23 +90,39 @@
         return mine,w
     for t in range(n//2):
         p0,p1=2*t,2*t+1
-        c0={q:[col_all(W[q],8*p0+k) for k in range(8)] for q in range(p0,n)}
+        near=range(p1+1,min(p1+1+NEAR,n)); far=range(min(p1+1+NEAR,n),n)
+        c0={q:[col_all(W[q],8*p0+k) for k in range(8)] for q in (p0,p1)}
         d1=[col_all(W[p1],8*p1+k) for k in range(8)]
+        c0.update({q:[col_all(W[q],8*p0+k) for k in range(8)] for q in near})
+        old=list(W)
         rs,l=small_chol(entries([x+zero for x in c0[p0]]))
         x=forward(c0[p1],rs,l)
         d1=[d1[k]-tree_sum([x[s]*row_all(x[s],k) for s in range(8)]) for k in range(8)]
-        mine,w=finish(p0,rs,l)
-        W[p1]=jnp.where(mine,0.0,W[p1])-tree_sum([x[s]*w[s] for s in range(8)])
-        v=backward(w,rs,l)
-        for q in range(p1+1,n):
-            W[q]=jnp.where(mine,0.0,W[q])-tree_sum([c0[q][s]*v[s] for s in range(8)])
+        mine0,w=finish(p0,rs,l)
+        W[p1]=jnp.where(mine0,0.0,W[p1])-tree_sum([x[s]*w[s] for s in range(8)])
+        v0=backward(w,rs,l)
+        for q in near:
+            W[q]=jnp.where(mine0,0.0,W[q])-tree_sum([c0[q][s]*v0[s] for s in range(8)])
         rs,l=small_chol(entries(d1))
-        c1={q:[col_all(W[q],8*p1+k) for k in range(8)] for q in range(p1+1,n)}
-        mine,w=finish(p1,rs,l)
-        v=backward(w,rs,l)
-        for q in range(p1+1,n):
-            W[q]=jnp.where(mine,0.0,W[q])-tree_sum([c1[q][s]*v[s] for s in range(8)])
+        c1={q:[col_all(W[q],8*p1+k) for k in range(8)] for q in near}
+        mine1,w=finish(p1,rs,l)
+        v1=backward(w,rs,l)
+        for q in near:
+            W[q]=jnp.where(mine1,0.0,W[q])-tree_sum([c1[q][s]*v1[s] for s in range(8)])
+        if len(far):
+            def pick(v):
+                o=v[7]
+                for s in range(6,-1,-1): o=jnp.where(sub==s,v[s],o)
+                return o
+            V0=pick(v0); V1=pick(v1)
+            V0=jnp.where(mine1,0.0,V0)-tree_sum([col_all(V0,8*p1+k)*v1[k] for k in range(8)])
+            z=jnp.zeros(REG,jnp.float32)
+            rhs=jnp.concatenate([z]*p0+[V0,V1]+[z]*(n-p1-1),0)
+            prod=lax.dot_general(jnp.concatenate([old[q] for q in far],0),rhs,(((1,),(0,)),((),())),precision=lax.Precision.HIGHEST,preferred_element_type=jnp.float32)
+            for i,q in enumerate(far):
+                W[q]=jnp.where(mine0|mine1,0.0,W[q])-prod[8*i:8*i+8]
     return G
+
 
 def unpack_points(packed):
     n = packed.shape[0] // 16
@@ -105,6 +136,23 @@
     middle = rest.astype(jnp.bfloat16)
     low = (rest - middle.astype(jnp.float32)).astype(jnp.bfloat16)
     return high, middle, low
+
+
+def stacked(a, b):
+    n = a.shape[0]
+    high, middle, low = split(a)
+    b = split(b)
+    first = dot16(jnp.concatenate([high, middle, low], axis=0), b[0], NN)
+    second = dot16(jnp.concatenate([high, middle], axis=0), b[1], NN)
+    small = first[2 * n :] + second[n:] + dot16(high, b[2], NN)
+    return first[0:n] + (first[n : 2 * n] + second[0:n] + small)
+
+
+def chained(a, b):
+    a, b = split(a), split(b)
+    left = jnp.concatenate([a[i] for i in (0, 0, 1, 1, 0, 2)], axis=1)
+    right = jnp.concatenate([b[i] for i in (0, 1, 0, 1, 2, 0)], axis=0)
+    return dot16(left, right, NN)
 
 
 def spread_terms(parts, order, values, axis):
@@ -140,13 +188,15 @@
 
 
 def panel_kernel(
-    where_ref, pan_ref, look_ref, scales_ref, zero_ref, rows_ref, weight_ref,
+    pan_ref, look_ref, scales_ref, rows_ref,
     diag_ref, panel_ref, update_ref,
-    z_ref, left_ref, a_ref, g_ref, b_ref, right_ref, kern_ref,
+    z_ref, left_ref, a_ref, g_ref, b_ref, right_ref, kern_ref, weight_ref,
 ):
     nb = B // TILE
-    col, row = where_ref[0], where_ref[1]
+    col, row = lax.axis_index("col"), lax.axis_index("row")
     scales = scales_ref[...]
+    weight_ref[...] = jnp.broadcast_to(jnp.broadcast_to(scales, (8, F)).T[:, 0:1], (F, TILE))
+    zero = jnp.full(REG, jnp.minimum(col, 0).astype(jnp.float32))
     points = unpack_points(pan_ref[...])
     look = unpack_points(look_ref[...])
     share = look.shape[0]
@@ -168,7 +218,7 @@
 
     def after_tile(k):
         here = slice(k * TILE, (k + 1) * TILE)
-        a_ref[here, k * TILE :] = mm(g_ref[k], a_ref[here, k * TILE :], NN)
+        a_ref[here, k * TILE :] = chained(g_ref[k], a_ref[here, k * TILE :])
         if k % 2 == 0:
             later = slice((k + 1) * TILE, (k + 2) * TILE)
             a_ref[later, later.start :] -= mm(a_ref[here, later], a_ref[here, later.start :], TN)
@@ -180,12 +230,12 @@
 
     def step(k, carry):
         at = pl.multiple_of(k * TILE, TILE)
-        G = factor_tile([a_ref[pl.ds(at + 8 * q, 8), pl.ds(at, TILE)] for q in range(TILE // 8)], zero_ref[...])
+        G = factor_tile([a_ref[pl.ds(at + 8 * q, 8), pl.ds(at, TILE)] for q in range(TILE // 8)], zero)
         for q in range(TILE // 8):
             g_ref[k, 8 * q : 8 * q + 8, :] = G[q]
         to = pl.ds(pl.multiple_of(k * wide, wide), wide)
         rows = rows_ref[:, to]
-        sq = jnp.sum(rows * rows * weight_ref[...], axis=0, keepdims=True)
+        sq = jnp.sum(rows * rows * weight_ref[:, 0:1], axis=0, keepdims=True)
         kern_ref[:, to] = jnp.exp(dot16(left_ref[...], right_terms(rows, sq, 0), NN))
         lax.switch(k, [functools.partial(after_tile, i) for i in range(nb)])
         return carry
@@ -216,7 +266,7 @@
 
     def product(j, carry):
         to = pl.ds(pl.multiple_of(j * block, block), block)
-        both = mm(z_ref[...], kern_ref[0:B, to], NN)
+        both = stacked(z_ref[...], kern_ref[0:B, to])
         panel_ref[:, to] = both[0:share]
         update_ref[:, to] = kern_ref[B : B + share, to] - both[share : 2 * share]
         return carry
@@ -224,22 +274,20 @@
     lax.fori_loop(0, rows_ref.shape[1] // block, product, 0)
 
 
-def pack(points):
-    rows = points.T
-    return jnp.concatenate([rows[0:16], rows[16:32]], axis=1)
-
-
-def local(where, panel, look, scales, row_points):
+def pack(points, copies):
+    rows = jnp.broadcast_to(points.T, (copies,) + points.shape[::-1])
+    return jnp.concatenate([rows[:, 0:16], rows[:, 16:32]], axis=2)
+
+
+def local(panel, look, scales, row_points):
     share = 2 * look.shape[0]
     rows_dev = row_points.shape[1]
-    scales_row = scales.reshape(1, F)
-    scales_col = scales.reshape(F, 1)
     vmem = pl.BlockSpec(memory_space=pltpu.VMEM)
     out = jax.ShapeDtypeStruct((share, rows_dev), jnp.float32)
     diag, panel_tile, updated = pl.pallas_call(
         panel_kernel,
         out_shape=(jax.ShapeDtypeStruct((share, B // 8), jnp.float32), out, out),
-        in_specs=[pl.BlockSpec(memory_space=pltpu.SMEM)] + [vmem] * 6,
+        in_specs=[vmem] * 4,
         out_specs=(vmem, vmem, vmem),
         scratch_shapes=[
             pltpu.VMEM((2 * share, B), jnp.float32),
@@ -249,9 +297,10 @@
             pltpu.VMEM((2 * share, B), jnp.float32),
             pltpu.VMEM((B + TILE, 4 * TILE), jnp.bfloat16),
             pltpu.VMEM((B + share, rows_dev), jnp.float32),
+            pltpu.VMEM((F, TILE), jnp.float32),
         ],
         name="panel",
-    )(where, panel, look, scales_row, jnp.zeros(REG, jnp.float32), row_points, scales_col)
+    )(panel, look, scales.reshape(1, F), row_points)
     return (diag.T, panel_tile, updated)
 
 
@@ -263,14 +312,12 @@
     share = B // n_col
     rows_dev = row_points.shape[1]
     first = col * share
-    own = pack(panel_points)
-    panel = lax.all_to_all(jnp.broadcast_to(own, (n_col,) + own.shape), "col", 0, 0, tiled=True)
+    panel = lax.all_to_all(pack(panel_points, n_col), "col", 0, 0, tiled=True)
     panel = panel.reshape(B // 2, 2 * F)
-    look = pack(lax.dynamic_slice_in_dim(row_points, first % rows_dev, share, 1))
+    look = pack(lax.dynamic_slice_in_dim(row_points, first % rows_dev, share, 1), 1)[0]
     sent = [lax.ppermute(look, "row", [(0, to)]) for to in range(1, n_row)]
     look = jnp.where(row == 0, look, sum(sent[1:], sent[0]))
-    where = jnp.stack([col, row]).astype(jnp.int32)
-    return local(where, panel, look, scales, row_points)
+    return local(panel, look, scales, row_points)
 
 
 def solution(mesh):

time: 80.2 us -> 73.8 us (0.920)
  Pallas kernels: 49.5 us -> 43.3 us
  local copies, waits for them, and re-layouts: 4.39 us -> 2.37 us
  waiting for transfers between devices: 6.36 us -> 8.34 us
    pallas_call x1, Pallas kernels: 49.5 us -> 43.3 us  [local(): pl.pallas_call(panel_kernel, out_shape=(jax.ShapeDtypeStruct((share, B //...]
    ppermute x7, waiting for transfers between devices: 6.35 us -> 8.34 us  [body(): sent = [lax.ppermute(look, 'row', [(0, to)]) for to in range(1, n_row)]]
    broadcast_in_dim x2, local copies, waits for them, and re-layouts: 1.33 us -> 0.04 us  [pack(): rows = jnp.broadcast_to(points.T, (copies,) + points.shape[::-1])]
  transfers between devices with their start and end apart: 8 -> 8, of which waited for: 1 -> 1; matrix products, arithmetic and copies ran while one was open for 4% -> 2% of each run, Pallas kernels for 0% -> 0%
where the time goes in v4:
time: 73.8 us; the launch traced here: 73.4 us
  Pallas kernels  43.3 us (59%)
  starting transfers between devices  17.1 us (23%)
  waiting for transfers between devices  8.34 us (11%)
  local copies, waits for them, and re-layouts  2.37 us (3%)
  other arithmetic  1.52 us (2%)
  between operations  0.78 us (1%)
    pallas_call x1, Pallas kernels, local(): pl.pallas_call(panel_kernel, out_shape=(jax.ShapeDtypeStruct((share, B //...  43.3 us
    all_to_all x1, starting transfers between devices, body(): panel = lax.all_to_all(pack(panel_points, n_col), 'col', 0, 0, tiled=True)  11.9 us
    ppermute x7, waiting for transfers between devices, body(): sent = [lax.ppermute(look, 'row', [(0, to)]) for to in range(1, n_row)]  8.34 us
    ppermute x7, starting transfers between devices, body(): sent = [lax.ppermute(look, 'row', [(0, to)]) for to in range(1, n_row)]  5.26 us
  transfers between devices with their start and end apart: 8, of which 1 were waited for; matrix products, arithmetic and copies ran while one was open for 2% of the time, Pallas kernels for 0%

profile of v4, /device:TPU:1, one launch (start us, length us, event | category | flops | bytes accessed | tf_op | source)
XLA Modules:
  0.0 73.4 jit_solution(15850261623128074385)
XLA Ops:
  0.6 0.7 fusion.1
  1.4 0.8 %pad_maximum_fusion = f32[32,16,128]{2,1,0:T(8,128)} fusion(f32[32,16,64]{2,1,0:T(8,128)S(1)} %broadcast_in_dim.9, f32[32,16,64]{2,1,0:T(8,128)S(1)} %broadcast_in_dim.8), kind=kLoop, calls=%fused_computation | loop fusion | flops 65536 | bytes 524288 | tf_op jit(solution)/shard_map/concatenate | solution.py:279
  2.2 11.9 %all-to-all-start = ((f32[32,16,128]{2,1,0:T(8,128)}), f32[32,16,128]{2,1,0:T(8,128)S(1)}, u32[]{:S(2)}, u32[]{:S(2)}) async-start(f32[32,16,128]{2,1,0:T(8,128)} %pad_maximum_fusion), calls=%async_computation | async-start | bytes 524288 | tf_op jit(solution)/shard_map/all_to_all | solution.py:315
  14.1 0.8 %constant_dynamic-slice_fusion = f32[64,32]{1,0:T(8,128)S(1)} fusion(f32[64,2048]{1,0:T(8,128)} %rows_ref.1, s32[]{:T(128)S(6)} %select_n.20), kind=kLoop, calls=%fused_computation.3 | loop fusion | bytes 16388 | tf_op jit(solution)/shard_map/dynamic_slice | solution.py:317
  15.0 0.1 copy.7
  15.0 0.1 maximum_bitcast_fusion
  15.1 0.7 collective-permute-start.6
  15.8 0.7 collective-permute-start.5
  16.5 0.7 collective-permute-start.4
  17.1 0.7 collective-permute-start.3
  17.8 0.7 collective-permute-start.2
  18.5 0.0 collective-permute-done.6
  18.5 0.7 collective-permute-start.1
  19.1 0.0 collective-permute-done.5
  19.2 1.3 %collective-permute-start = (f32[16,128]{1,0:T(8,128)S(1)}, f32[16,128]{1,0:T(8,128)S(1)}, u32[]{:S(2)}, u32[]{:S(2)}) collective-permute-start(f32[16,128]{1,0:T(8,128)S(1)} %maximum_bitcast_fusion), channel_id=1, source_target_pairs={{0,32},{1,33},{2,34},{3,35},{4,36},{5,37},{6,38},{7,39},{8,40},{9,... | collective-permute-start | bytes 24584 | tf_op jit(solution)/shard_map/ppermute | solution.py:318
  20.5 0.0 collective-permute-done.4
  20.5 0.0 collective-permute-done.3
  20.5 0.0 collective-permute-done.2
  20.5 0.0 collective-permute-done.1
  20.5 8.3 %collective-permute-done = f32[16,128]{1,0:T(8,128)S(1)} collective-permute-done((f32[16,128]{1,0:T(8,128)S(1)}, f32[16,128]{1,0:T(8,128)S(1)}, u32[]{:S(2)}, u32[]{:S(2)}) %collective-permute-start) | collective-permute-done | bytes 8224 | tf_op jit(solution)/shard_map/ppermute | solution.py:318
  28.8 0.6 add_select_fusion.look_ref
  29.4 0.0 all-to-all-done
  29.4 0.0 copy-start
  29.4 0.7 copy-done
  30.1 43.3 %panel.1 = (f32[32,128]{1,0:T(8,128)}, f32[32,2048]{1,0:T(8,128)}, f32[32,2048]{1,0:T(8,128)}) custom-call(f32[512,128]{1,0:T(8,128)} %bitcast.9, f32[16,128]{1,0:T(8,128)} %add_select_fusion.look_ref, f32[1,64]{1,0:T(1,128)} %bitcast.12, f32[64,2048]{1,0:T(8,128)} %rows_ref.1), custom_call_target="tpu_custom_call" | custom-call | tf_op jit(solution)/shard_map/panel/pallas_call | solution.py:287
  (3 shorter events, 0.0 us)
Async XLA Ops:
  2.2 27.2 %all-to-all-start = ((f32[32,16,128]{2,1,0:T(8,128)}), f32[32,16,128]{2,1,0:T(8,128)S(1)}, u32[]{:S(2)}, u32[]{:S(2)}) async-start(f32[32,16,128]{2,1,0:T(8,128)} %pad_maximum_fusion), calls=%async_computation | async-start | bytes 524288 | tf_op jit(solution)/shard_map/all_to_all | solution.py:315
  15.1 3.4 %collective-permute-start.6 = (f32[16,128]{1,0:T(8,128)S(1)}, f32[16,128]{1,0:T(8,128)S(1)}, u32[]{:S(2)}, u32[]{:S(2)}) collective-permute-start(f32[16,128]{1,0:T(8,128)S(1)} %maximum_bitcast_fusion), channel_id=1, source_target_pairs={{0,224},{1,225},{2,226},{3,227},{4,228},{5,229},{6,230},{7,231},{8... | collective-permute-start | bytes 24584 | tf_op jit(solution)/shard_map/ppermute | solution.py:318
  15.8 3.4 %collective-permute-start.5 = (f32[16,128]{1,0:T(8,128)S(1)}, f32[16,128]{1,0:T(8,128)S(1)}, u32[]{:S(2)}, u32[]{:S(2)}) collective-permute-start(f32[16,128]{1,0:T(8,128)S(1)} %maximum_bitcast_fusion), channel_id=1, source_target_pairs={{0,192},{1,193},{2,194},{3,195},{4,196},{5,197},{6,198},{7,199},{8... | collective-permute-start | bytes 24584 | tf_op jit(solution)/shard_map/ppermute | solution.py:318
  16.5 4.0 %collective-permute-start.4 = (f32[16,128]{1,0:T(8,128)S(1)}, f32[16,128]{1,0:T(8,128)S(1)}, u32[]{:S(2)}, u32[]{:S(2)}) collective-permute-start(f32[16,128]{1,0:T(8,128)S(1)} %maximum_bitcast_fusion), channel_id=1, source_target_pairs={{0,160},{1,161},{2,162},{3,163},{4,164},{5,165},{6,166},{7,167},{8... | collective-permute-start | bytes 24584 | tf_op jit(solution)/shard_map/ppermute | solution.py:318
  17.1 3.3 %collective-permute-start.3 = (f32[16,128]{1,0:T(8,128)S(1)}, f32[16,128]{1,0:T(8,128)S(1)}, u32[]{:S(2)}, u32[]{:S(2)}) collective-permute-start(f32[16,128]{1,0:T(8,128)S(1)} %maximum_bitcast_fusion), channel_id=1, source_target_pairs={{0,128},{1,129},{2,130},{3,131},{4,132},{5,133},{6,134},{7,135},{8... | collective-permute-start | bytes 24584 | tf_op jit(solution)/shard_map/ppermute | solution.py:318
  17.8 2.7 %collective-permute-start.2 = (f32[16,128]{1,0:T(8,128)S(1)}, f32[16,128]{1,0:T(8,128)S(1)}, u32[]{:S(2)}, u32[]{:S(2)}) collective-permute-start(f32[16,128]{1,0:T(8,128)S(1)} %maximum_bitcast_fusion), channel_id=1, source_target_pairs={{0,96},{1,97},{2,98},{3,99},{4,100},{5,101},{6,102},{7,103},{8,104... | collective-permute-start | bytes 24584 | tf_op jit(solution)/shard_map/ppermute | solution.py:318
  18.5 2.0 %collective-permute-start.1 = (f32[16,128]{1,0:T(8,128)S(1)}, f32[16,128]{1,0:T(8,128)S(1)}, u32[]{:S(2)}, u32[]{:S(2)}) collective-permute-start(f32[16,128]{1,0:T(8,128)S(1)} %maximum_bitcast_fusion), channel_id=1, source_target_pairs={{0,64},{1,65},{2,66},{3,67},{4,68},{5,69},{6,70},{7,71},{8,72},{9,... | collective-permute-start | bytes 24584 | tf_op jit(solution)/shard_map/ppermute | solution.py:318
  19.2 9.7 %collective-permute-start = (f32[16,128]{1,0:T(8,128)S(1)}, f32[16,128]{1,0:T(8,128)S(1)}, u32[]{:S(2)}, u32[]{:S(2)}) collective-permute-start(f32[16,128]{1,0:T(8,128)S(1)} %maximum_bitcast_fusion), channel_id=1, source_target_pairs={{0,32},{1,33},{2,34},{3,35},{4,36},{5,37},{6,38},{7,39},{8,40},{9,... | collective-permute-start | bytes 24584 | tf_op jit(solution)/shard_map/ppermute | solution.py:318
  29.4 0.7 copy-start

commit v5 on v4

--- a/solution.py
+++ b/solution.py
@@ -39,28 +39,21 @@
     return xs[0]
 
 def small_chol(d):
-    d=[list(x) for x in d]
+    d=list(d)
     rs=[None]*8; l=[[None]*8 for _ in range(8)]
     for s in range(0,8,2):
-        a,b,c=d[s][s],d[s+1][s],d[s+1][s+1]
+        a,b,c=row_all(d[s],s),row_all(d[s],s+1),row_all(d[s+1],s+1)
         det=a*c-b*b
-        r0=lax.rsqrt(a)
-        l10=b*r0
-        rd=lax.rsqrt(det)
-        inv=rd*rd
-        r1=(a*r0)*rd
-        r01=r0*rd
-        rs[s]=r0; rs[s+1]=r1
-        l[s+1][s]=l10
-        y0={};y1={}
-        for k in range(s+2,8):
-            y0[k]=c*d[k][s]-b*d[k][s+1]
-            y1[k]=a*d[k][s+1]-b*d[k][s]
-            l[k][s]=d[k][s]*r0
-            l[k][s+1]=y1[k]*r01
-        for k in range(s+2,8):
-            for m in range(s+2,k+1):
-                d[k][m]=d[k][m]-(y0[k]*d[m][s]+y1[k]*d[m][s+1])*inv
+        r0=lax.rsqrt(a); rd=lax.rsqrt(det); inv=rd*rd
+        rs[s]=r0; rs[s+1]=(a*r0)*rd
+        y1=a*d[s+1]-b*d[s]
+        l0=d[s]*r0; l1=y1*(r0*rd)
+        for k in range(s+1,8): l[k][s]=row_all(l0,k)
+        for k in range(s+2,8): l[k][s+1]=row_all(l1,k)
+        if s<6:
+            y0=c*d[s]-b*d[s+1]
+            for m in range(s+2,8):
+                d[m]=d[m]-(y0*row_all(d[s],m)+y1*row_all(d[s+1],m))*inv
     return rs,l
 def forward(x,rs,l):
     x=list(x)
@@ -79,7 +72,6 @@
     n=len(W); W=list(W)
     sub=lax.broadcasted_iota(jnp.int32,REG,0); lane=lax.broadcasted_iota(jnp.int32,REG,1)
     G=[None]*n
-    def entries(cols): return [[row_all(cols[k],i) if i>=k else None for k in range(8)] for i in range(8)]
     def finish(p, rs, l):
         mine=lax.shift_right_logical(lane,3)==p
         w=jnp.where(mine, jnp.where(lane-8*p==sub,1.0,0.0).astype(jnp.float32), W[p])
@@ -95,7 +87,7 @@
         d1=[col_all(W[p1],8*p1+k) for k in range(8)]
         c0.update({q:[col_all(W[q],8*p0+k) for k in range(8)] for q in near})
         old=list(W)
-        rs,l=small_chol(entries([x+zero for x in c0[p0]]))
+        rs,l=small_chol([x+zero for x in c0[p0]])
         x=forward(c0[p1],rs,l)
         d1=[d1[k]-tree_sum([x[s]*row_all(x[s],k) for s in range(8)]) for k in range(8)]
         mine0,w=finish(p0,rs,l)
@@ -103,7 +95,7 @@
         v0=backward(w,rs,l)
         for q in near:
             W[q]=jnp.where(mine0,0.0,W[q])-tree_sum([c0[q][s]*v0[s] for s in range(8)])
-        rs,l=small_chol(entries(d1))
+        rs,l=small_chol(d1)
         c1={q:[col_all(W[q],8*p1+k) for k in range(8)] for q in near}
         mine1,w=finish(p1,rs,l)
         v1=backward(w,rs,l)
@@ -138,13 +130,13 @@
     return high, middle, low
 
 
-def stacked(a, b):
+def stacked(a, b, dims=NN):
     n = a.shape[0]
     high, middle, low = split(a)
     b = split(b)
-    first = dot16(jnp.concatenate([high, middle, low], axis=0), b[0], NN)
-    second = dot16(jnp.concatenate([high, middle], axis=0), b[1], NN)
-    small = first[2 * n :] + second[n:] + dot16(high, b[2], NN)
+    first = dot16(jnp.concatenate([high, middle, low], axis=0), b[0], dims)
+    second = dot16(jnp.concatenate([high, middle], axis=0), b[1], dims)
+    small = first[2 * n :] + second[n:] + dot16(high, b[2], dims)
     return first[0:n] + (first[n : 2 * n] + second[0:n] + small)
 
 
@@ -250,10 +242,10 @@
         b_ref[share : 2 * share, cols] = a_ref[cols, B : B + TILE].T[0:share, :]
     for k in range(nb - 1, -1, -1):
         cols = slice(k * TILE, (k + 1) * TILE)
-        z = mm(b_ref[:, cols], g_ref[k], NN)
+        z = stacked(b_ref[:, cols], g_ref[k])
         z_ref[:, cols] = z
         if k > 0:
-            b_ref[:, 0 : k * TILE] = b_ref[:, 0 : k * TILE] - mm(z, a_ref[0 : k * TILE, cols], NT)
+            b_ref[:, 0 : k * TILE] = b_ref[:, 0 : k * TILE] - stacked(z, a_ref[0 : k * TILE, cols], NT)
 
     own = pl.ds(pl.multiple_of(col * share, share), share)
     to = pl.multiple_of(row * TILE, TILE)

time: 73.8 us -> 70.5 us (0.955)
  Pallas kernels: 43.3 us -> 39.9 us
    pallas_call x1, Pallas kernels: 43.3 us -> 39.9 us  [local(): pl.pallas_call(panel_kernel, out_shape=(jax.ShapeDtypeStruct((share, B //...]
where the time goes in v5:
time: 70.5 us; the launch traced here: 70.1 us
  Pallas kernels  39.9 us (57%)
  starting transfers between devices  17.1 us (24%)
  waiting for transfers between devices  8.34 us (12%)
  local copies, waits for them, and re-layouts  2.37 us (3%)
  other arithmetic  1.52 us (2%)
  between operations  0.78 us (1%)
    pallas_call x1, Pallas kernels, local(): pl.pallas_call(panel_kernel, out_shape=(jax.ShapeDtypeStruct((share, B //...  39.9 us
    all_to_all x1, starting transfers between devices, body(): panel = lax.all_to_all(pack(panel_points, n_col), 'col', 0, 0, tiled=True)  11.9 us
    ppermute x7, waiting for transfers between devices, body(): sent = [lax.ppermute(look, 'row', [(0, to)]) for to in range(1, n_row)]  8.34 us
    ppermute x7, starting transfers between devices, body(): sent = [lax.ppermute(look, 'row', [(0, to)]) for to in range(1, n_row)]  5.26 us
  transfers between devices with their start and end apart: 8, of which 1 were waited for; matrix products, arithmetic and copies ran while one was open for 2% of the time, Pallas kernels for 0%

profile of v5, /device:TPU:1, one launch (start us, length us, event | category | flops | bytes accessed | tf_op | source)
XLA Modules:
  0.0 70.1 jit_solution(17296196820598261175)
XLA Ops:
  0.6 0.7 %fusion.1 = (f32[16,64]{1,0:T(8,128)S(1)}, f32[16,64]{1,0:T(8,128)S(1)}) fusion(f32[32,64]{1,0:T(8,128)} %bitcast.11), kind=kLoop, calls=%fused_computation.5 | loop fusion | bytes 16384 | tf_op jit(solution)/shard_map/slice | solution.py:271
  1.4 0.8 %pad_maximum_fusion = f32[32,16,128]{2,1,0:T(8,128)} fusion(f32[32,16,64]{2,1,0:T(8,128)S(1)} %broadcast_in_dim.9, f32[32,16,64]{2,1,0:T(8,128)S(1)} %broadcast_in_dim.8), kind=kLoop, calls=%fused_computation | loop fusion | flops 65536 | bytes 524288 | tf_op jit(solution)/shard_map/concatenate | solution.py:271
  2.2 11.9 %all-to-all-start = ((f32[32,16,128]{2,1,0:T(8,128)}), f32[32,16,128]{2,1,0:T(8,128)S(1)}, u32[]{:S(2)}, u32[]{:S(2)}) async-start(f32[32,16,128]{2,1,0:T(8,128)} %pad_maximum_fusion), calls=%async_computation | async-start | bytes 524288 | tf_op jit(solution)/shard_map/all_to_all | solution.py:307
  14.1 0.8 %constant_dynamic-slice_fusion = f32[64,32]{1,0:T(8,128)S(1)} fusion(f32[64,2048]{1,0:T(8,128)} %rows_ref.1, s32[]{:T(128)S(6)} %select_n.20), kind=kLoop, calls=%fused_computation.3 | loop fusion | bytes 16388 | tf_op jit(solution)/shard_map/dynamic_slice | solution.py:309
  15.0 0.1 copy.7
  15.0 0.1 maximum_bitcast_fusion
  15.1 0.7 collective-permute-start.6
  15.8 0.7 collective-permute-start.5
  16.5 0.7 collective-permute-start.4
  17.1 0.7 collective-permute-start.3
  17.8 0.7 collective-permute-start.2
  18.5 0.0 collective-permute-done.6
  18.5 0.7 collective-permute-start.1
  19.1 0.0 collective-permute-done.5
  19.2 1.3 %collective-permute-start = (f32[16,128]{1,0:T(8,128)S(1)}, f32[16,128]{1,0:T(8,128)S(1)}, u32[]{:S(2)}, u32[]{:S(2)}) collective-permute-start(f32[16,128]{1,0:T(8,128)S(1)} %maximum_bitcast_fusion), channel_id=1, source_target_pairs={{0,32},{1,33},{2,34},{3,35},{4,36},{5,37},{6,38},{7,39},{8,40},{9,... | collective-permute-start | bytes 24584 | tf_op jit(solution)/shard_map/ppermute | solution.py:310
  20.5 0.0 collective-permute-done.4
  20.5 0.0 collective-permute-done.3
  20.5 0.0 collective-permute-done.2
  20.5 0.0 collective-permute-done.1
  20.5 8.3 %collective-permute-done = f32[16,128]{1,0:T(8,128)S(1)} collective-permute-done((f32[16,128]{1,0:T(8,128)S(1)}, f32[16,128]{1,0:T(8,128)S(1)}, u32[]{:S(2)}, u32[]{:S(2)}) %collective-permute-start) | collective-permute-done | bytes 8224 | tf_op jit(solution)/shard_map/ppermute | solution.py:310
  28.8 0.6 add_select_fusion.look_ref
  29.4 0.0 all-to-all-done
  29.4 0.0 copy-start
  29.4 0.7 %copy-done = f32[32,16,128]{2,1,0:T(8,128)} copy-done((f32[32,16,128]{2,1,0:T(8,128)}, f32[32,16,128]{2,1,0:T(8,128)S(1)}, u32[]{:S(2)}) %copy-start) | copy-done | bytes 262168
  30.1 39.9 %panel.1 = (f32[32,128]{1,0:T(8,128)}, f32[32,2048]{1,0:T(8,128)}, f32[32,2048]{1,0:T(8,128)}) custom-call(f32[512,128]{1,0:T(8,128)} %bitcast.9, f32[16,128]{1,0:T(8,128)} %add_select_fusion.look_ref, f32[1,64]{1,0:T(1,128)} %bitcast.12, f32[64,2048]{1,0:T(8,128)} %rows_ref.1), custom_call_target="tpu_custom_call" | custom-call | tf_op jit(solution)/shard_map/panel/pallas_call | solution.py:279
  (3 shorter events, 0.0 us)
Async XLA Ops:
  2.2 27.2 %all-to-all-start = ((f32[32,16,128]{2,1,0:T(8,128)}), f32[32,16,128]{2,1,0:T(8,128)S(1)}, u32[]{:S(2)}, u32[]{:S(2)}) async-start(f32[32,16,128]{2,1,0:T(8,128)} %pad_maximum_fusion), calls=%async_computation | async-start | bytes 524288 | tf_op jit(solution)/shard_map/all_to_all | solution.py:307
  15.1 3.4 %collective-permute-start.6 = (f32[16,128]{1,0:T(8,128)S(1)}, f32[16,128]{1,0:T(8,128)S(1)}, u32[]{:S(2)}, u32[]{:S(2)}) collective-permute-start(f32[16,128]{1,0:T(8,128)S(1)} %maximum_bitcast_fusion), channel_id=1, source_target_pairs={{0,224},{1,225},{2,226},{3,227},{4,228},{5,229},{6,230},{7,231},{8... | collective-permute-start | bytes 24584 | tf_op jit(solution)/shard_map/ppermute | solution.py:310
  15.8 3.4 %collective-permute-start.5 = (f32[16,128]{1,0:T(8,128)S(1)}, f32[16,128]{1,0:T(8,128)S(1)}, u32[]{:S(2)}, u32[]{:S(2)}) collective-permute-start(f32[16,128]{1,0:T(8,128)S(1)} %maximum_bitcast_fusion), channel_id=1, source_target_pairs={{0,192},{1,193},{2,194},{3,195},{4,196},{5,197},{6,198},{7,199},{8... | collective-permute-start | bytes 24584 | tf_op jit(solution)/shard_map/ppermute | solution.py:310
  16.5 4.0 %collective-permute-start.4 = (f32[16,128]{1,0:T(8,128)S(1)}, f32[16,128]{1,0:T(8,128)S(1)}, u32[]{:S(2)}, u32[]{:S(2)}) collective-permute-start(f32[16,128]{1,0:T(8,128)S(1)} %maximum_bitcast_fusion), channel_id=1, source_target_pairs={{0,160},{1,161},{2,162},{3,163},{4,164},{5,165},{6,166},{7,167},{8... | collective-permute-start | bytes 24584 | tf_op jit(solution)/shard_map/ppermute | solution.py:310
  17.1 3.3 %collective-permute-start.3 = (f32[16,128]{1,0:T(8,128)S(1)}, f32[16,128]{1,0:T(8,128)S(1)}, u32[]{:S(2)}, u32[]{:S(2)}) collective-permute-start(f32[16,128]{1,0:T(8,128)S(1)} %maximum_bitcast_fusion), channel_id=1, source_target_pairs={{0,128},{1,129},{2,130},{3,131},{4,132},{5,133},{6,134},{7,135},{8... | collective-permute-start | bytes 24584 | tf_op jit(solution)/shard_map/ppermute | solution.py:310
  17.8 2.7 %collective-permute-start.2 = (f32[16,128]{1,0:T(8,128)S(1)}, f32[16,128]{1,0:T(8,128)S(1)}, u32[]{:S(2)}, u32[]{:S(2)}) collective-permute-start(f32[16,128]{1,0:T(8,128)S(1)} %maximum_bitcast_fusion), channel_id=1, source_target_pairs={{0,96},{1,97},{2,98},{3,99},{4,100},{5,101},{6,102},{7,103},{8,104... | collective-permute-start | bytes 24584 | tf_op jit(solution)/shard_map/ppermute | solution.py:310
  18.5 2.0 %collective-permute-start.1 = (f32[16,128]{1,0:T(8,128)S(1)}, f32[16,128]{1,0:T(8,128)S(1)}, u32[]{:S(2)}, u32[]{:S(2)}) collective-permute-start(f32[16,128]{1,0:T(8,128)S(1)} %maximum_bitcast_fusion), channel_id=1, source_target_pairs={{0,64},{1,65},{2,66},{3,67},{4,68},{5,69},{6,70},{7,71},{8,72},{9,... | collective-permute-start | bytes 24584 | tf_op jit(solution)/shard_map/ppermute | solution.py:310
  19.2 9.7 %collective-permute-start = (f32[16,128]{1,0:T(8,128)S(1)}, f32[16,128]{1,0:T(8,128)S(1)}, u32[]{:S(2)}, u32[]{:S(2)}) collective-permute-start(f32[16,128]{1,0:T(8,128)S(1)} %maximum_bitcast_fusion), channel_id=1, source_target_pairs={{0,32},{1,33},{2,34},{3,35},{4,36},{5,37},{6,38},{7,39},{8,40},{9,... | collective-permute-start | bytes 24584 | tf_op jit(solution)/shard_map/ppermute | solution.py:310
  29.4 0.7 %copy-start = (f32[32,16,128]{2,1,0:T(8,128)}, f32[32,16,128]{2,1,0:T(8,128)S(1)}, u32[]{:S(2)}) copy-start(f32[32,16,128]{2,1,0:T(8,128)S(1)} %all-to-all-done) | copy-start | bytes 786436

commit v6 on v5

--- a/solution.py
+++ b/solution.py
@@ -92,8 +92,11 @@
         d1=[d1[k]-tree_sum([x[s]*row_all(x[s],k) for s in range(8)]) for k in range(8)]
         mine0,w=finish(p0,rs,l)
         W[p1]=jnp.where(mine0,0.0,W[p1])-tree_sum([x[s]*w[s] for s in range(8)])
+        for q in near[:2]:
+            y=forward(c0[q],rs,l)
+            W[q]=jnp.where(mine0,0.0,W[q])-tree_sum([y[s]*w[s] for s in range(8)])
         v0=backward(w,rs,l)
-        for q in near:
+        for q in near[2:]:
             W[q]=jnp.where(mine0,0.0,W[q])-tree_sum([c0[q][s]*v0[s] for s in range(8)])
         rs,l=small_chol(d1)
         c1={q:[col_all(W[q],8*p1+k) for k in range(8)] for q in near}
@@ -307,8 +310,10 @@
     panel = lax.all_to_all(pack(panel_points, n_col), "col", 0, 0, tiled=True)
     panel = panel.reshape(B // 2, 2 * F)
     look = pack(lax.dynamic_slice_in_dim(row_points, first % rows_dev, share, 1), 1)[0]
-    sent = [lax.ppermute(look, "row", [(0, to)]) for to in range(1, n_row)]
+    sent = [lax.ppermute(look, "row", [(0, to)]) for to in range(n_row - 2, 0, -2)]
     look = jnp.where(row == 0, look, sum(sent[1:], sent[0]))
+    next_row = lax.ppermute(look, "row", [(i, i + 1) for i in range(0, n_row, 2)])
+    look = jnp.where(row % 2 == 0, look, next_row)
     return local(panel, look, scales, row_points)
 
 

time: 70.5 us -> 68.2 us (0.967)
  starting transfers between devices: 17.1 us -> 15.1 us
    ppermute x7 -> x4, starting transfers between devices: 5.26 us -> 3.28 us  [the longest x3 1.99 us: body(): lax.ppermute(look, 'row', [(0, to)])]
    ppermute x7 -> x4, waiting for transfers between devices: 8.34 us -> 7.95 us  [the longest x1 7.94 us: body(): lax.ppermute(look, 'row', [(i, i + 1) for i in range(0, n_row, 2)])]
  transfers between devices with their start and end apart: 8 -> 5, of which waited for: 1 -> 1; matrix products, arithmetic and copies ran while one was open for 2% -> 2% of each run, Pallas kernels for 0% -> 0%
where the time goes in v6:
time: 68.2 us; the launch traced here: 67.9 us
  Pallas kernels  40.1 us (59%)
  starting transfers between devices  15.1 us (22%)
  waiting for transfers between devices  7.95 us (12%)
  local copies, waits for them, and re-layouts  2.36 us (3%)
  other arithmetic  1.53 us (2%)
  between operations  0.75 us (1%)
    pallas_call x1, Pallas kernels, local(): pl.pallas_call(panel_kernel, out_shape=(jax.ShapeDtypeStruct((share, B //...  40.1 us
    all_to_all x1, starting transfers between devices, body(): panel = lax.all_to_all(pack(panel_points, n_col), 'col', 0, 0, tiled=True)  11.9 us
    ppermute x1, waiting for transfers between devices, body(): lax.ppermute(look, 'row', [(i, i + 1) for i in range(0, n_row, 2)])  7.94 us
    ppermute x3, starting transfers between devices, body(): lax.ppermute(look, 'row', [(0, to)])  1.99 us
  transfers between devices with their start and end apart: 5, of which 1 were waited for; matrix products, arithmetic and copies ran while one was open for 2% of the time, Pallas kernels for 0%

profile of v6, /device:TPU:1, one launch (start us, length us, event | category | flops | bytes accessed | tf_op | source)
XLA Modules:
  0.0 67.9 jit_solution(8888316883711006499)
XLA Ops:
  0.6 0.7 %fusion.1 = (f32[16,64]{1,0:T(8,128)S(1)}, f32[16,64]{1,0:T(8,128)S(1)}) fusion(f32[32,64]{1,0:T(8,128)} %bitcast.11), kind=kLoop, calls=%fused_computation.6 | loop fusion | bytes 16384 | tf_op jit(solution)/shard_map/slice | solution.py:274
  1.4 0.8 %pad_maximum_fusion = f32[32,16,128]{2,1,0:T(8,128)} fusion(f32[32,16,64]{2,1,0:T(8,128)S(1)} %broadcast_in_dim.9, f32[32,16,64]{2,1,0:T(8,128)S(1)} %broadcast_in_dim.8), kind=kLoop, calls=%fused_computation | loop fusion | flops 65536 | bytes 524288 | tf_op jit(solution)/shard_map/concatenate | solution.py:274
  2.2 11.9 %all-to-all-start = ((f32[32,16,128]{2,1,0:T(8,128)}), f32[32,16,128]{2,1,0:T(8,128)S(1)}, u32[]{:S(2)}, u32[]{:S(2)}) async-start(f32[32,16,128]{2,1,0:T(8,128)} %pad_maximum_fusion), calls=%async_computation | async-start | bytes 524288 | tf_op jit(solution)/shard_map/all_to_all | solution.py:310
  14.1 0.8 %constant_dynamic-slice_fusion = f32[64,32]{1,0:T(8,128)S(1)} fusion(f32[64,2048]{1,0:T(8,128)} %rows_ref.1, s32[]{:T(128)S(6)} %select_n.32), kind=kLoop, calls=%fused_computation.4 | loop fusion | bytes 16388 | tf_op jit(solution)/shard_map/dynamic_slice | solution.py:312
  15.0 0.1 copy.7
  15.0 0.1 maximum_bitcast_fusion
  15.1 0.7 collective-permute-start.2
  15.8 0.7 collective-permute-start.1
  16.5 0.7 collective-permute-start
  17.1 0.0 collective-permute-done.2
  17.1 0.0 collective-permute-done.1
  17.2 0.0 collective-permute-done
  17.2 1.3 %collective-permute-start.3 = (f32[16,128]{1,0:T(8,128)S(1)}, f32[16,128]{1,0:T(8,128)S(1)}, u32[]{:S(2)}, u32[]{:S(2)}) collective-permute-start(f32[16,128]{1,0:T(8,128)S(1)} %add_select_fusion), channel_id=1, source_target_pairs={{0,32},{64,96},{128,160},{192,224},{1,33},{65,97},{129,161},{193,2... | collective-permute-start | bytes 24584 | tf_op jit(solution)/shard_map/ppermute | solution.py:315
  18.5 7.9 %collective-permute-done.3 = f32[16,128]{1,0:T(8,128)S(1)} collective-permute-done((f32[16,128]{1,0:T(8,128)S(1)}, f32[16,128]{1,0:T(8,128)S(1)}, u32[]{:S(2)}, u32[]{:S(2)}) %collective-permute-start.3) | collective-permute-done | bytes 8224 | tf_op jit(solution)/shard_map/ppermute | solution.py:315
  26.4 0.6 broadcast_select_fusion.look_ref
  27.0 0.0 all-to-all-done
  27.0 0.0 copy-start
  27.0 0.7 %copy-done = f32[32,16,128]{2,1,0:T(8,128)} copy-done((f32[32,16,128]{2,1,0:T(8,128)}, f32[32,16,128]{2,1,0:T(8,128)S(1)}, u32[]{:S(2)}) %copy-start) | copy-done | bytes 262168
  27.7 40.1 %panel.1 = (f32[32,128]{1,0:T(8,128)}, f32[32,2048]{1,0:T(8,128)}, f32[32,2048]{1,0:T(8,128)}) custom-call(f32[512,128]{1,0:T(8,128)} %bitcast.9, f32[16,128]{1,0:T(8,128)} %broadcast_select_fusion.look_ref, f32[1,64]{1,0:T(1,128)} %bitcast.12, f32[64,2048]{1,0:T(8,128)} %rows_ref.1), custom_call_target="tpu_custom_call" | custom-call | tf_op jit(solution)/shard_map/panel/pallas_call | solution.py:282
  (4 shorter events, 0.1 us)
Async XLA Ops:
  2.2 24.8 %all-to-all-start = ((f32[32,16,128]{2,1,0:T(8,128)}), f32[32,16,128]{2,1,0:T(8,128)S(1)}, u32[]{:S(2)}, u32[]{:S(2)}) async-start(f32[32,16,128]{2,1,0:T(8,128)} %pad_maximum_fusion), calls=%async_computation | async-start | bytes 524288 | tf_op jit(solution)/shard_map/all_to_all | solution.py:310
  15.1 2.0 %collective-permute-start.2 = (f32[16,128]{1,0:T(8,128)S(1)}, f32[16,128]{1,0:T(8,128)S(1)}, u32[]{:S(2)}, u32[]{:S(2)}) collective-permute-start(f32[16,128]{1,0:T(8,128)S(1)} %maximum_bitcast_fusion), channel_id=1, source_target_pairs={{0,64},{1,65},{2,66},{3,67},{4,68},{5,69},{6,70},{7,71},{8,72},{9,... | collective-permute-start | bytes 24584 | tf_op jit(solution)/shard_map/ppermute | solution.py:313
  15.8 1.4 %collective-permute-start.1 = (f32[16,128]{1,0:T(8,128)S(1)}, f32[16,128]{1,0:T(8,128)S(1)}, u32[]{:S(2)}, u32[]{:S(2)}) collective-permute-start(f32[16,128]{1,0:T(8,128)S(1)} %maximum_bitcast_fusion), channel_id=1, source_target_pairs={{0,128},{1,129},{2,130},{3,131},{4,132},{5,133},{6,134},{7,135},{8... | collective-permute-start | bytes 24584 | tf_op jit(solution)/shard_map/ppermute | solution.py:313
  16.5 0.7 %collective-permute-start = (f32[16,128]{1,0:T(8,128)S(1)}, f32[16,128]{1,0:T(8,128)S(1)}, u32[]{:S(2)}, u32[]{:S(2)}) collective-permute-start(f32[16,128]{1,0:T(8,128)S(1)} %maximum_bitcast_fusion), channel_id=1, source_target_pairs={{0,192},{1,193},{2,194},{3,195},{4,196},{5,197},{6,198},{7,199},{8... | collective-permute-start | bytes 24584 | tf_op jit(solution)/shard_map/ppermute | solution.py:313
  17.2 9.3 %collective-permute-start.3 = (f32[16,128]{1,0:T(8,128)S(1)}, f32[16,128]{1,0:T(8,128)S(1)}, u32[]{:S(2)}, u32[]{:S(2)}) collective-permute-start(f32[16,128]{1,0:T(8,128)S(1)} %add_select_fusion), channel_id=1, source_target_pairs={{0,32},{64,96},{128,160},{192,224},{1,33},{65,97},{129,161},{193,2... | collective-permute-start | bytes 24584 | tf_op jit(solution)/shard_map/ppermute | solution.py:315
  27.0 0.7 %copy-start = (f32[32,16,128]{2,1,0:T(8,128)}, f32[32,16,128]{2,1,0:T(8,128)S(1)}, u32[]{:S(2)}) copy-start(f32[32,16,128]{2,1,0:T(8,128)S(1)} %all-to-all-done) | copy-start | bytes 786436

commit v7 on v6

--- a/solution.py
+++ b/solution.py
@@ -150,13 +150,13 @@
     return dot16(left, right, NN)
 
 
-def spread_terms(parts, order, values, axis):
+def spread_terms(parts, order, values, first_one, axis):
     shape = list(parts[0].shape)
     shape[axis] = TILE
     place = lax.broadcasted_iota(jnp.int32, shape, axis)
-    tail = jnp.zeros(shape, jnp.float32)
+    tail = jnp.where((place >= first_one) & (place < first_one + 3), 1.0, 0.0).astype(jnp.float32)
     for i, v in enumerate(values):
-        tail = jnp.where(place == i, v, tail)
+        tail = jnp.where(place == 3 - first_one + i, v, tail)
     return jnp.concatenate([parts[i] for i in order] + [tail.astype(jnp.bfloat16)], axis=axis)
 
 
@@ -171,11 +171,11 @@
 def left_terms(points, scales):
     weighted = points * scales
     sq = jnp.sum(weighted * points, axis=1, keepdims=True)
-    return spread_terms(split(2.0 * weighted), LEFT, as_float(split(-sq)) + [1.0, 1.0, 1.0], 1)
+    return spread_terms(split(2.0 * weighted), LEFT, as_float(split(-sq)), 3, 1)
 
 
 def right_terms(points, sq, axis):
-    return spread_terms(split(points), RIGHT, [1.0, 1.0, 1.0] + as_float(split(-sq)), axis)
+    return spread_terms(split(points), RIGHT, as_float(split(-sq)), 0, axis)
 
 
 def dot16(a, b, dims):
@@ -271,7 +271,9 @@
 
 def pack(points, copies):
     rows = jnp.broadcast_to(points.T, (copies,) + points.shape[::-1])
-    return jnp.concatenate([rows[:, 0:16], rows[:, 16:32]], axis=2)
+    first = lax.pad(rows, 0.0, ((0, 0, 0), (0, -16, 0), (0, F, 0)))
+    second = lax.pad(rows, 0.0, ((0, 0, 0), (-16, 0, 0), (F, 0, 0)))
+    return first + second
 
 
 def local(panel, look, scales, row_points):

time: 68.2 us -> 68.3 us (level)
    add x0 -> x1, other arithmetic: none -> 0.84 us  [pack(): return first + second]
    concatenate x1 -> x0, other arithmetic: 0.84 us -> none  [pack(): return jnp.concatenate([rows[:, 0:16], rows[:, 16:32]], axis=2)]
    broadcast_in_dim x2 -> x1, local copies, waits for them, and re-layouts: 0.04 us -> 0.77 us  [pack(): rows = jnp.broadcast_to(points.T, (copies,) + points.shape[::-1])]
    slice x2 -> x0, local copies, waits for them, and re-layouts: 0.72 us -> none  [pack(): return jnp.concatenate([rows[:, 0:16], rows[:, 16:32]], axis=2)]
where the time goes in v7:
time: 68.3 us; the launch traced here: 67.9 us
  Pallas kernels  40.1 us (59%)
  starting transfers between devices  15.1 us (22%)
  waiting for transfers between devices  7.97 us (12%)
  local copies, waits for them, and re-layouts  2.37 us (3%)
  other arithmetic  1.6 us (2%)
  between operations  0.74 us (1%)
    pallas_call x1, Pallas kernels, local(): pl.pallas_call(panel_kernel, out_shape=(jax.ShapeDtypeStruct((share, B //...  40.1 us
    all_to_all x1, starting transfers between devices, body(): panel = lax.all_to_all(pack(panel_points, n_col), 'col', 0, 0, tiled=True)  11.9 us
    ppermute x1, waiting for transfers between devices, body(): lax.ppermute(look, 'row', [(i, i + 1) for i in range(0, n_row, 2)])  7.96 us
    ppermute x3, starting transfers between devices, body(): lax.ppermute(look, 'row', [(0, to)])  1.99 us
  transfers between devices with their start and end apart: 5, of which 1 were waited for; matrix products, arithmetic and copies ran while one was open for 2% of the time, Pallas kernels for 0%

profile of v7, /device:TPU:1, one launch (start us, length us, event | category | flops | bytes accessed | tf_op | source)
XLA Modules:
  0.0 67.9 jit_solution(771003184562168859)
XLA Ops:
  0.6 0.8 %broadcast_in_dim.6 = f32[32,32,64]{2,1,0:T(8,128)S(1)} broadcast(f32[32,64]{1,0:T(8,128)} %bitcast.14), dimensions={1,2} | broadcast | bytes 270336 | tf_op jit(solution)/shard_map/broadcast_in_dim | solution.py:273
  1.4 0.8 %fusion = f32[32,16,128]{2,1,0:T(8,128)} fusion(f32[32,32,64]{2,1,0:T(8,128)S(1)} %broadcast_in_dim.6), kind=kLoop, calls=%fused_computation.2 | loop fusion | flops 65536 | bytes 524288 | tf_op jit(solution)/shard_map/add | solution.py:276
  2.2 11.9 %all-to-all-start = ((f32[32,16,128]{2,1,0:T(8,128)}), f32[32,16,128]{2,1,0:T(8,128)S(1)}, u32[]{:S(2)}, u32[]{:S(2)}) async-start(f32[32,16,128]{2,1,0:T(8,128)} %fusion), calls=%async_computation | async-start | bytes 524288 | tf_op jit(solution)/shard_map/all_to_all | solution.py:312
  14.1 0.8 %constant_dynamic-slice_fusion = f32[64,32]{1,0:T(8,128)S(1)} fusion(f32[64,2048]{1,0:T(8,128)} %rows_ref.1, s32[]{:T(128)S(6)} %select_n.32), kind=kLoop, calls=%fused_computation.9 | loop fusion | bytes 16388 | tf_op jit(solution)/shard_map/dynamic_slice | solution.py:314
  15.0 0.1 copy.7
  15.0 0.1 fusion.2
  15.1 0.7 collective-permute-start.2
  15.8 0.7 collective-permute-start.1
  16.5 0.7 collective-permute-start
  17.1 0.0 collective-permute-done.2
  17.2 0.0 collective-permute-done.1
  17.2 0.0 collective-permute-done
  17.2 0.1 add_select_fusion
  17.3 1.3 %collective-permute-start.3 = (f32[16,128]{1,0:T(8,128)S(1)}, f32[16,128]{1,0:T(8,128)S(1)}, u32[]{:S(2)}, u32[]{:S(2)}) collective-permute-start(f32[16,128]{1,0:T(8,128)S(1)} %add_select_fusion), channel_id=1, source_target_pairs={{0,32},{64,96},{128,160},{192,224},{1,33},{65,97},{129,161},{193,2... | collective-permute-start | bytes 24584 | tf_op jit(solution)/shard_map/ppermute | solution.py:317
  18.6 8.0 %collective-permute-done.3 = f32[16,128]{1,0:T(8,128)S(1)} collective-permute-done((f32[16,128]{1,0:T(8,128)S(1)}, f32[16,128]{1,0:T(8,128)S(1)}, u32[]{:S(2)}, u32[]{:S(2)}) %collective-permute-start.3) | collective-permute-done | bytes 8224 | tf_op jit(solution)/shard_map/ppermute | solution.py:317
  26.5 0.6 broadcast_select_fusion.look_ref
  27.1 0.0 all-to-all-done
  27.1 0.0 copy-start
  27.1 0.7 %copy-done = f32[32,16,128]{2,1,0:T(8,128)} copy-done((f32[32,16,128]{2,1,0:T(8,128)}, f32[32,16,128]{2,1,0:T(8,128)S(1)}, u32[]{:S(2)}) %copy-start) | copy-done | bytes 262168
  27.8 40.1 %panel.1 = (f32[32,128]{1,0:T(8,128)}, f32[32,2048]{1,0:T(8,128)}, f32[32,2048]{1,0:T(8,128)}) custom-call(f32[512,128]{1,0:T(8,128)} %bitcast.11, f32[16,128]{1,0:T(8,128)} %broadcast_select_fusion.look_ref, f32[1,64]{1,0:T(1,128)} %bitcast.15, f32[64,2048]{1,0:T(8,128)} %rows_ref.1), custom_call_target="tpu_custom_call" | custom-call | tf_op jit(solution)/shard_map/panel/pallas_call | solution.py:284
Async XLA Ops:
  2.2 24.9 %all-to-all-start = ((f32[32,16,128]{2,1,0:T(8,128)}), f32[32,16,128]{2,1,0:T(8,128)S(1)}, u32[]{:S(2)}, u32[]{:S(2)}) async-start(f32[32,16,128]{2,1,0:T(8,128)} %fusion), calls=%async_computation | async-start | bytes 524288 | tf_op jit(solution)/shard_map/all_to_all | solution.py:312
  15.1 2.0 %collective-permute-start.2 = (f32[16,128]{1,0:T(8,128)S(1)}, f32[16,128]{1,0:T(8,128)S(1)}, u32[]{:S(2)}, u32[]{:S(2)}) collective-permute-start(f32[16,128]{1,0:T(8,128)S(1)} %fusion.2), channel_id=1, source_target_pairs={{0,64},{1,65},{2,66},{3,67},{4,68},{5,69},{6,70},{7,71},{8,72},{9,... | collective-permute-start | bytes 24584 | tf_op jit(solution)/shard_map/ppermute | solution.py:315
  15.8 1.4 %collective-permute-start.1 = (f32[16,128]{1,0:T(8,128)S(1)}, f32[16,128]{1,0:T(8,128)S(1)}, u32[]{:S(2)}, u32[]{:S(2)}) collective-permute-start(f32[16,128]{1,0:T(8,128)S(1)} %fusion.2), channel_id=1, source_target_pairs={{0,128},{1,129},{2,130},{3,131},{4,132},{5,133},{6,134},{7,135},{8... | collective-permute-start | bytes 24584 | tf_op jit(solution)/shard_map/ppermute | solution.py:315
  16.5 0.7 %collective-permute-start = (f32[16,128]{1,0:T(8,128)S(1)}, f32[16,128]{1,0:T(8,128)S(1)}, u32[]{:S(2)}, u32[]{:S(2)}) collective-permute-start(f32[16,128]{1,0:T(8,128)S(1)} %fusion.2), channel_id=1, source_target_pairs={{0,192},{1,193},{2,194},{3,195},{4,196},{5,197},{6,198},{7,199},{8... | collective-permute-start | bytes 24584 | tf_op jit(solution)/shard_map/ppermute | solution.py:315
  17.3 9.3 %collective-permute-start.3 = (f32[16,128]{1,0:T(8,128)S(1)}, f32[16,128]{1,0:T(8,128)S(1)}, u32[]{:S(2)}, u32[]{:S(2)}) collective-permute-start(f32[16,128]{1,0:T(8,128)S(1)} %add_select_fusion), channel_id=1, source_target_pairs={{0,32},{64,96},{128,160},{192,224},{1,33},{65,97},{129,161},{193,2... | collective-permute-start | bytes 24584 | tf_op jit(solution)/shard_map/ppermute | solution.py:317
  27.1 0.7 %copy-start = (f32[32,16,128]{2,1,0:T(8,128)}, f32[32,16,128]{2,1,0:T(8,128)S(1)}, u32[]{:S(2)}) copy-start(f32[32,16,128]{2,1,0:T(8,128)S(1)} %all-to-all-done) | copy-start | bytes 786436

commit v8 on v5

--- a/solution.py
+++ b/solution.py
@@ -83,7 +83,9 @@
     for t in range(n//2):
         p0,p1=2*t,2*t+1
         near=range(p1+1,min(p1+1+NEAR,n)); far=range(min(p1+1+NEAR,n),n)
-        c0={q:[col_all(W[q],8*p0+k) for k in range(8)] for q in (p0,p1)}
+        c0={p0:[],p1:[]}
+        for k in range(8):
+            c0[p0].append(col_all(W[p0],8*p0+k)); c0[p1].append(col_all(W[p1],8*p0+k))
         d1=[col_all(W[p1],8*p1+k) for k in range(8)]
         c0.update({q:[col_all(W[q],8*p0+k) for k in range(8)] for q in near})
         old=list(W)
@@ -307,8 +309,10 @@
     panel = lax.all_to_all(pack(panel_points, n_col), "col", 0, 0, tiled=True)
     panel = panel.reshape(B // 2, 2 * F)
     look = pack(lax.dynamic_slice_in_dim(row_points, first % rows_dev, share, 1), 1)[0]
-    sent = [lax.ppermute(look, "row", [(0, to)]) for to in range(1, n_row)]
+    sent = [lax.ppermute(look, "row", [(0, to)]) for to in range(n_row - 2, 0, -2)]
     look = jnp.where(row == 0, look, sum(sent[1:], sent[0]))
+    next_row = lax.ppermute(look, "row", [(i, i + 1) for i in range(0, n_row, 2)])
+    look = jnp.where(row % 2 == 0, look, next_row)
     return local(panel, look, scales, row_points)
 
 

time: 70.5 us -> 68 us (0.965)
  starting transfers between devices: 17.1 us -> 15.1 us
    ppermute x7 -> x4, starting transfers between devices: 5.26 us -> 3.28 us  [the longest x3 1.99 us: body(): lax.ppermute(look, 'row', [(0, to)])]
    ppermute x7 -> x4, waiting for transfers between devices: 8.34 us -> 7.95 us  [the longest x1 7.94 us: body(): lax.ppermute(look, 'row', [(i, i + 1) for i in range(0, n_row, 2)])]
  transfers between devices with their start and end apart: 8 -> 5, of which waited for: 1 -> 1; matrix products, arithmetic and copies ran while one was open for 2% -> 2% of each run, Pallas kernels for 0% -> 0%
where the time goes in v8:
time: 68 us; the launch traced here: 67.7 us
  Pallas kernels  39.9 us (59%)
  starting transfers between devices  15.1 us (22%)
  waiting for transfers between devices  7.95 us (12%)
  local copies, waits for them, and re-layouts  2.36 us (3%)
  other arithmetic  1.53 us (2%)
  between operations  0.75 us (1%)
    pallas_call x1, Pallas kernels, local(): pl.pallas_call(panel_kernel, out_shape=(jax.ShapeDtypeStruct((share, B //...  39.9 us
    all_to_all x1, starting transfers between devices, body(): panel = lax.all_to_all(pack(panel_points, n_col), 'col', 0, 0, tiled=True)  11.9 us
    ppermute x1, waiting for transfers between devices, body(): lax.ppermute(look, 'row', [(i, i + 1) for i in range(0, n_row, 2)])  7.94 us
    ppermute x3, starting transfers between devices, body(): lax.ppermute(look, 'row', [(0, to)])  1.99 us
  transfers between devices with their start and end apart: 5, of which 1 were waited for; matrix products, arithmetic and copies ran while one was open for 2% of the time, Pallas kernels for 0%

profile of v8, /device:TPU:1, one launch (start us, length us, event | category | flops | bytes accessed | tf_op | source)
XLA Modules:
  0.0 67.7 jit_solution(5329413832380972775)
XLA Ops:
  0.6 0.7 %fusion.1 = (f32[16,64]{1,0:T(8,128)S(1)}, f32[16,64]{1,0:T(8,128)S(1)}) fusion(f32[32,64]{1,0:T(8,128)} %bitcast.11), kind=kLoop, calls=%fused_computation.6 | loop fusion | bytes 16384 | tf_op jit(solution)/shard_map/slice | solution.py:273
  1.4 0.8 %pad_maximum_fusion = f32[32,16,128]{2,1,0:T(8,128)} fusion(f32[32,16,64]{2,1,0:T(8,128)S(1)} %broadcast_in_dim.9, f32[32,16,64]{2,1,0:T(8,128)S(1)} %broadcast_in_dim.8), kind=kLoop, calls=%fused_computation | loop fusion | flops 65536 | bytes 524288 | tf_op jit(solution)/shard_map/concatenate | solution.py:273
  2.2 11.9 %all-to-all-start = ((f32[32,16,128]{2,1,0:T(8,128)}), f32[32,16,128]{2,1,0:T(8,128)S(1)}, u32[]{:S(2)}, u32[]{:S(2)}) async-start(f32[32,16,128]{2,1,0:T(8,128)} %pad_maximum_fusion), calls=%async_computation | async-start | bytes 524288 | tf_op jit(solution)/shard_map/all_to_all | solution.py:309
  14.1 0.8 %constant_dynamic-slice_fusion = f32[64,32]{1,0:T(8,128)S(1)} fusion(f32[64,2048]{1,0:T(8,128)} %rows_ref.1, s32[]{:T(128)S(6)} %select_n.32), kind=kLoop, calls=%fused_computation.4 | loop fusion | bytes 16388 | tf_op jit(solution)/shard_map/dynamic_slice | solution.py:311
  15.0 0.1 copy.7
  15.0 0.1 maximum_bitcast_fusion
  15.1 0.7 collective-permute-start.2
  15.8 0.7 collective-permute-start.1
  16.5 0.7 collective-permute-start
  17.1 0.0 collective-permute-done.2
  17.1 0.0 collective-permute-done.1
  17.2 0.0 collective-permute-done
  17.2 1.3 %collective-permute-start.3 = (f32[16,128]{1,0:T(8,128)S(1)}, f32[16,128]{1,0:T(8,128)S(1)}, u32[]{:S(2)}, u32[]{:S(2)}) collective-permute-start(f32[16,128]{1,0:T(8,128)S(1)} %add_select_fusion), channel_id=1, source_target_pairs={{0,32},{64,96},{128,160},{192,224},{1,33},{65,97},{129,161},{193,2... | collective-permute-start | bytes 24584 | tf_op jit(solution)/shard_map/ppermute | solution.py:314
  18.5 7.9 %collective-permute-done.3 = f32[16,128]{1,0:T(8,128)S(1)} collective-permute-done((f32[16,128]{1,0:T(8,128)S(1)}, f32[16,128]{1,0:T(8,128)S(1)}, u32[]{:S(2)}, u32[]{:S(2)}) %collective-permute-start.3) | collective-permute-done | bytes 8224 | tf_op jit(solution)/shard_map/ppermute | solution.py:314
  26.4 0.6 broadcast_select_fusion.look_ref
  27.0 0.0 all-to-all-done
  27.0 0.0 copy-start
  27.0 0.7 %copy-done = f32[32,16,128]{2,1,0:T(8,128)} copy-done((f32[32,16,128]{2,1,0:T(8,128)}, f32[32,16,128]{2,1,0:T(8,128)S(1)}, u32[]{:S(2)}) %copy-start) | copy-done | bytes 262168
  27.7 39.9 %panel.1 = (f32[32,128]{1,0:T(8,128)}, f32[32,2048]{1,0:T(8,128)}, f32[32,2048]{1,0:T(8,128)}) custom-call(f32[512,128]{1,0:T(8,128)} %bitcast.9, f32[16,128]{1,0:T(8,128)} %broadcast_select_fusion.look_ref, f32[1,64]{1,0:T(1,128)} %bitcast.12, f32[64,2048]{1,0:T(8,128)} %rows_ref.1), custom_call_target="tpu_custom_call" | custom-call | tf_op jit(solution)/shard_map/panel/pallas_call | solution.py:281
  (4 shorter events, 0.1 us)
Async XLA Ops:
  2.2 24.8 %all-to-all-start = ((f32[32,16,128]{2,1,0:T(8,128)}), f32[32,16,128]{2,1,0:T(8,128)S(1)}, u32[]{:S(2)}, u32[]{:S(2)}) async-start(f32[32,16,128]{2,1,0:T(8,128)} %pad_maximum_fusion), calls=%async_computation | async-start | bytes 524288 | tf_op jit(solution)/shard_map/all_to_all | solution.py:309
  15.1 2.0 %collective-permute-start.2 = (f32[16,128]{1,0:T(8,128)S(1)}, f32[16,128]{1,0:T(8,128)S(1)}, u32[]{:S(2)}, u32[]{:S(2)}) collective-permute-start(f32[16,128]{1,0:T(8,128)S(1)} %maximum_bitcast_fusion), channel_id=1, source_target_pairs={{0,64},{1,65},{2,66},{3,67},{4,68},{5,69},{6,70},{7,71},{8,72},{9,... | collective-permute-start | bytes 24584 | tf_op jit(solution)/shard_map/ppermute | solution.py:312
  15.8 1.4 %collective-permute-start.1 = (f32[16,128]{1,0:T(8,128)S(1)}, f32[16,128]{1,0:T(8,128)S(1)}, u32[]{:S(2)}, u32[]{:S(2)}) collective-permute-start(f32[16,128]{1,0:T(8,128)S(1)} %maximum_bitcast_fusion), channel_id=1, source_target_pairs={{0,128},{1,129},{2,130},{3,131},{4,132},{5,133},{6,134},{7,135},{8... | collective-permute-start | bytes 24584 | tf_op jit(solution)/shard_map/ppermute | solution.py:312
  16.5 0.7 %collective-permute-start = (f32[16,128]{1,0:T(8,128)S(1)}, f32[16,128]{1,0:T(8,128)S(1)}, u32[]{:S(2)}, u32[]{:S(2)}) collective-permute-start(f32[16,128]{1,0:T(8,128)S(1)} %maximum_bitcast_fusion), channel_id=1, source_target_pairs={{0,192},{1,193},{2,194},{3,195},{4,196},{5,197},{6,198},{7,199},{8... | collective-permute-start | bytes 24584 | tf_op jit(solution)/shard_map/ppermute | solution.py:312
  17.2 9.3 %collective-permute-start.3 = (f32[16,128]{1,0:T(8,128)S(1)}, f32[16,128]{1,0:T(8,128)S(1)}, u32[]{:S(2)}, u32[]{:S(2)}) collective-permute-start(f32[16,128]{1,0:T(8,128)S(1)} %add_select_fusion), channel_id=1, source_target_pairs={{0,32},{64,96},{128,160},{192,224},{1,33},{65,97},{129,161},{193,2... | collective-permute-start | bytes 24584 | tf_op jit(solution)/shard_map/ppermute | solution.py:314
  27.0 0.7 %copy-start = (f32[32,16,128]{2,1,0:T(8,128)}, f32[32,16,128]{2,1,0:T(8,128)S(1)}, u32[]{:S(2)}) copy-start(f32[32,16,128]{2,1,0:T(8,128)S(1)} %all-to-all-done) | copy-start | bytes 786436

commit v9 on v8

--- a/solution.py
+++ b/solution.py
@@ -182,7 +182,7 @@
 
 
 def panel_kernel(
-    pan_ref, look_ref, scales_ref, rows_ref,
+    pan_ref, look_ref, sent_ref, scales_ref, rows_ref,
     diag_ref, panel_ref, update_ref,
     z_ref, left_ref, a_ref, g_ref, b_ref, right_ref, kern_ref, weight_ref,
 ):
@@ -192,7 +192,7 @@
     weight_ref[...] = jnp.broadcast_to(jnp.broadcast_to(scales, (8, F)).T[:, 0:1], (F, TILE))
     zero = jnp.full(REG, jnp.minimum(col, 0).astype(jnp.float32))
     points = unpack_points(pan_ref[...])
-    look = unpack_points(look_ref[...])
+    look = unpack_points(jnp.where(row % 2 == 0, look_ref[...], sent_ref[...]))
     share = look.shape[0]
     left_ref[0:B] = left_terms(points, scales)
     left_ref[B : B + share] = left_terms(look, scales)
@@ -273,7 +273,7 @@
     return jnp.concatenate([rows[:, 0:16], rows[:, 16:32]], axis=2)
 
 
-def local(panel, look, scales, row_points):
+def local(panel, look, sent_look, scales, row_points):
     share = 2 * look.shape[0]
     rows_dev = row_points.shape[1]
     vmem = pl.BlockSpec(memory_space=pltpu.VMEM)
@@ -281,7 +281,7 @@
     diag, panel_tile, updated = pl.pallas_call(
         panel_kernel,
         out_shape=(jax.ShapeDtypeStruct((share, B // 8), jnp.float32), out, out),
-        in_specs=[vmem] * 4,
+        in_specs=[vmem] * 5,
         out_specs=(vmem, vmem, vmem),
         scratch_shapes=[
             pltpu.VMEM((2 * share, B), jnp.float32),
@@ -294,7 +294,7 @@
             pltpu.VMEM((F, TILE), jnp.float32),
         ],
         name="panel",
-    )(panel, look, scales.reshape(1, F), row_points)
+    )(panel, look, sent_look, scales.reshape(1, F), row_points)
     return (diag.T, panel_tile, updated)
 
 
@@ -312,8 +312,7 @@
     sent = [lax.ppermute(look, "row", [(0, to)]) for to in range(n_row - 2, 0, -2)]
     look = jnp.where(row == 0, look, sum(sent[1:], sent[0]))
     next_row = lax.ppermute(look, "row", [(i, i + 1) for i in range(0, n_row, 2)])
-    look = jnp.where(row % 2 == 0, look, next_row)
-    return local(panel, look, scales, row_points)
+    return local(panel, look, next_row, scales, row_points)
 
 
 def solution(mesh):

time: 68 us -> 67.4 us (level)
  transfers between devices with their start and end apart: 5 -> 5, of which waited for: 1 -> 1; matrix products, arithmetic and copies ran while one was open for 2% -> 1% of each run, Pallas kernels for 0% -> 0%
where the time goes in v9:
time: 67.4 us; the launch traced here: 67.1 us
  Pallas kernels  39.9 us (59%)
  starting transfers between devices  15.1 us (22%)
  waiting for transfers between devices  7.96 us (12%)
  local copies, waits for them, and re-layouts  2.37 us (4%)
  other arithmetic  0.93 us (1%)
  between operations  0.75 us (1%)
    pallas_call x1, Pallas kernels, local(): pl.pallas_call(panel_kernel, out_shape=(jax.ShapeDtypeStruct((share, B //...  39.9 us
    all_to_all x1, starting transfers between devices, body(): panel = lax.all_to_all(pack(panel_points, n_col), 'col', 0, 0, tiled=True)  11.9 us
    ppermute x1, waiting for transfers between devices, body(): lax.ppermute(look, 'row', [(i, i + 1) for i in range(0, n_row, 2)])  7.95 us
    ppermute x3, starting transfers between devices, body(): lax.ppermute(look, 'row', [(0, to)])  1.99 us
  transfers between devices with their start and end apart: 5, of which 1 were waited for; matrix products, arithmetic and copies ran while one was open for 1% of the time, Pallas kernels for 0%

profile of v9, /device:TPU:1, one launch (start us, length us, event | category | flops | bytes accessed | tf_op | source)
XLA Modules:
  0.0 67.1 jit_solution(10841880959384148387)
XLA Ops:
  0.6 0.7 %fusion.1 = (f32[16,64]{1,0:T(8,128)S(1)}, f32[16,64]{1,0:T(8,128)S(1)}) fusion(f32[32,64]{1,0:T(8,128)} %bitcast.11), kind=kLoop, calls=%fused_computation.5 | loop fusion | bytes 16384 | tf_op jit(solution)/shard_map/slice | solution.py:273
  1.4 0.8 %pad_maximum_fusion = f32[32,16,128]{2,1,0:T(8,128)} fusion(f32[32,16,64]{2,1,0:T(8,128)S(1)} %broadcast_in_dim.9, f32[32,16,64]{2,1,0:T(8,128)S(1)} %broadcast_in_dim.8), kind=kLoop, calls=%fused_computation | loop fusion | flops 65536 | bytes 524288 | tf_op jit(solution)/shard_map/concatenate | solution.py:273
  2.2 11.9 %all-to-all-start = ((f32[32,16,128]{2,1,0:T(8,128)}), f32[32,16,128]{2,1,0:T(8,128)S(1)}, u32[]{:S(2)}, u32[]{:S(2)}) async-start(f32[32,16,128]{2,1,0:T(8,128)} %pad_maximum_fusion), calls=%async_computation | async-start | bytes 524288 | tf_op jit(solution)/shard_map/all_to_all | solution.py:309
  14.1 0.8 %constant_dynamic-slice_fusion = f32[64,32]{1,0:T(8,128)S(1)} fusion(f32[64,2048]{1,0:T(8,128)} %rows_ref.1, s32[]{:T(128)S(6)} %select_n.20), kind=kLoop, calls=%fused_computation.3 | loop fusion | bytes 16388 | tf_op jit(solution)/shard_map/dynamic_slice | solution.py:311
  15.0 0.1 copy.7
  15.0 0.1 maximum_bitcast_fusion
  15.1 0.7 collective-permute-start.2
  15.8 0.7 collective-permute-start.1
  16.5 0.7 collective-permute-start
  17.1 0.0 collective-permute-done.2
  17.1 0.0 collective-permute-done.1
  17.2 0.0 collective-permute-done
  17.2 0.0 copy-start.1
  17.2 1.3 %collective-permute-start.3 = (f32[16,128]{1,0:T(8,128)S(1)}, f32[16,128]{1,0:T(8,128)S(1)}, u32[]{:S(2)}, u32[]{:S(2)}) collective-permute-start(f32[16,128]{1,0:T(8,128)S(1)} %add_select_fusion.look_ref), channel_id=1, source_target_pairs={{0,32},{64,96},{128,160},{192,224},{1,33},{65,97},{129,161},{193,2... | collective-permute-start | bytes 24584 | tf_op jit(solution)/shard_map/ppermute | solution.py:314
  18.5 7.9 %collective-permute-done.3.sent_ref = f32[16,128]{1,0:T(8,128)S(1)} collective-permute-done((f32[16,128]{1,0:T(8,128)S(1)}, f32[16,128]{1,0:T(8,128)S(1)}, u32[]{:S(2)}, u32[]{:S(2)}) %collective-permute-start.3) | collective-permute-done | bytes 8224 | tf_op jit(solution)/shard_map/ppermute | solution.py:314
  26.4 0.0 copy-start.2
  26.4 0.0 all-to-all-done
  26.4 0.0 copy-start
  26.4 0.0 copy-done.1
  26.5 0.6 copy-done.2
  27.0 0.1 copy-done
  27.2 39.9 %panel.1 = (f32[32,128]{1,0:T(8,128)}, f32[32,2048]{1,0:T(8,128)}, f32[32,2048]{1,0:T(8,128)}) custom-call(f32[512,128]{1,0:T(8,128)} %bitcast.9, f32[16,128]{1,0:T(8,128)} %copy-done.1, f32[16,128]{1,0:T(8,128)} %copy-done.2, f32[1,64]{1,0:T(1,128)} %bitcast.12, f32[64,2048]{1,0:T(8,128)} %rows_ref.1), custom_call_target="tpu_custom_call" | custom-call | tf_op jit(solution)/shard_map/panel/pallas_call | solution.py:281
  (4 shorter events, 0.1 us)
Async XLA Ops:
  2.2 24.2 %all-to-all-start = ((f32[32,16,128]{2,1,0:T(8,128)}), f32[32,16,128]{2,1,0:T(8,128)S(1)}, u32[]{:S(2)}, u32[]{:S(2)}) async-start(f32[32,16,128]{2,1,0:T(8,128)} %pad_maximum_fusion), calls=%async_computation | async-start | bytes 524288 | tf_op jit(solution)/shard_map/all_to_all | solution.py:309
  15.1 2.0 %collective-permute-start.2 = (f32[16,128]{1,0:T(8,128)S(1)}, f32[16,128]{1,0:T(8,128)S(1)}, u32[]{:S(2)}, u32[]{:S(2)}) collective-permute-start(f32[16,128]{1,0:T(8,128)S(1)} %maximum_bitcast_fusion), channel_id=1, source_target_pairs={{0,64},{1,65},{2,66},{3,67},{4,68},{5,69},{6,70},{7,71},{8,72},{9,... | collective-permute-start | bytes 24584 | tf_op jit(solution)/shard_map/ppermute | solution.py:312
  15.8 1.4 %collective-permute-start.1 = (f32[16,128]{1,0:T(8,128)S(1)}, f32[16,128]{1,0:T(8,128)S(1)}, u32[]{:S(2)}, u32[]{:S(2)}) collective-permute-start(f32[16,128]{1,0:T(8,128)S(1)} %maximum_bitcast_fusion), channel_id=1, source_target_pairs={{0,128},{1,129},{2,130},{3,131},{4,132},{5,133},{6,134},{7,135},{8... | collective-permute-start | bytes 24584 | tf_op jit(solution)/shard_map/ppermute | solution.py:312
  16.5 0.7 %collective-permute-start = (f32[16,128]{1,0:T(8,128)S(1)}, f32[16,128]{1,0:T(8,128)S(1)}, u32[]{:S(2)}, u32[]{:S(2)}) collective-permute-start(f32[16,128]{1,0:T(8,128)S(1)} %maximum_bitcast_fusion), channel_id=1, source_target_pairs={{0,192},{1,193},{2,194},{3,195},{4,196},{5,197},{6,198},{7,199},{8... | collective-permute-start | bytes 24584 | tf_op jit(solution)/shard_map/ppermute | solution.py:312
  17.2 9.3 %copy-start.1 = (f32[16,128]{1,0:T(8,128)}, f32[16,128]{1,0:T(8,128)S(1)}, u32[]{:S(2)}) copy-start(f32[16,128]{1,0:T(8,128)S(1)} %add_select_fusion.look_ref) | copy-start | bytes 24580
  17.2 9.2 %collective-permute-start.3 = (f32[16,128]{1,0:T(8,128)S(1)}, f32[16,128]{1,0:T(8,128)S(1)}, u32[]{:S(2)}, u32[]{:S(2)}) collective-permute-start(f32[16,128]{1,0:T(8,128)S(1)} %add_select_fusion.look_ref), channel_id=1, source_target_pairs={{0,32},{64,96},{128,160},{192,224},{1,33},{65,97},{129,161},{193,2... | collective-permute-start | bytes 24584 | tf_op jit(solution)/shard_map/ppermute | solution.py:314
  26.4 0.6 copy-start.2
  26.4 0.7 %copy-start = (f32[32,16,128]{2,1,0:T(8,128)}, f32[32,16,128]{2,1,0:T(8,128)S(1)}, u32[]{:S(2)}) copy-start(f32[32,16,128]{2,1,0:T(8,128)S(1)} %all-to-all-done) | copy-start | bytes 786436

commit v10 on v9

--- a/solution.py
+++ b/solution.py
@@ -149,13 +149,13 @@
     return dot16(left, right, NN)
 
 
-def spread_terms(parts, order, values, axis):
+def spread_terms(parts, order, values, first_one, axis):
     shape = list(parts[0].shape)
     shape[axis] = TILE
     place = lax.broadcasted_iota(jnp.int32, shape, axis)
-    tail = jnp.zeros(shape, jnp.float32)
+    tail = jnp.where((place >= first_one) & (place < first_one + 3), 1.0, 0.0).astype(jnp.float32)
     for i, v in enumerate(values):
-        tail = jnp.where(place == i, v, tail)
+        tail = jnp.where(place == 3 - first_one + i, v, tail)
     return jnp.concatenate([parts[i] for i in order] + [tail.astype(jnp.bfloat16)], axis=axis)
 
 
@@ -170,11 +170,11 @@
 def left_terms(points, scales):
     weighted = points * scales
     sq = jnp.sum(weighted * points, axis=1, keepdims=True)
-    return spread_terms(split(2.0 * weighted), LEFT, as_float(split(-sq)) + [1.0, 1.0, 1.0], 1)
+    return spread_terms(split(2.0 * weighted), LEFT, as_float(split(-sq)), 3, 1)
 
 
 def right_terms(points, sq, axis):
-    return spread_terms(split(points), RIGHT, [1.0, 1.0, 1.0] + as_float(split(-sq)), axis)
+    return spread_terms(split(points), RIGHT, as_float(split(-sq)), 0, axis)
 
 
 def dot16(a, b, dims):

time: 67.4 us -> 67.4 us (level)
  no operation moved by 1% of the time
where the time goes in v10:
time: 67.4 us; the launch traced here: 67 us
  Pallas kernels  39.9 us (59%)
  starting transfers between devices  15.1 us (22%)
  waiting for transfers between devices  7.96 us (12%)
  local copies, waits for them, and re-layouts  2.37 us (4%)
  other arithmetic  0.93 us (1%)
  between operations  0.75 us (1%)
    pallas_call x1, Pallas kernels, local(): pl.pallas_call(panel_kernel, out_shape=(jax.ShapeDtypeStruct((share, B //...  39.9 us
    all_to_all x1, starting transfers between devices, body(): panel = lax.all_to_all(pack(panel_points, n_col), 'col', 0, 0, tiled=True)  11.9 us
    ppermute x1, waiting for transfers between devices, body(): lax.ppermute(look, 'row', [(i, i + 1) for i in range(0, n_row, 2)])  7.95 us
    ppermute x3, starting transfers between devices, body(): lax.ppermute(look, 'row', [(0, to)])  1.99 us
  transfers between devices with their start and end apart: 5, of which 1 were waited for; matrix products, arithmetic and copies ran while one was open for 1% of the time, Pallas kernels for 0%

profile of v10, /device:TPU:1, one launch (start us, length us, event | category | flops | bytes accessed | tf_op | source)
XLA Modules:
  0.0 67.0 jit_solution(12205553713636907843)
XLA Ops:
  0.6 0.7 %fusion.1 = (f32[16,64]{1,0:T(8,128)S(1)}, f32[16,64]{1,0:T(8,128)S(1)}) fusion(f32[32,64]{1,0:T(8,128)} %bitcast.11), kind=kLoop, calls=%fused_computation.5 | loop fusion | bytes 16384 | tf_op jit(solution)/shard_map/slice | solution.py:273
  1.4 0.8 %pad_maximum_fusion = f32[32,16,128]{2,1,0:T(8,128)} fusion(f32[32,16,64]{2,1,0:T(8,128)S(1)} %broadcast_in_dim.9, f32[32,16,64]{2,1,0:T(8,128)S(1)} %broadcast_in_dim.8), kind=kLoop, calls=%fused_computation | loop fusion | flops 65536 | bytes 524288 | tf_op jit(solution)/shard_map/concatenate | solution.py:273
  2.2 11.9 %all-to-all-start = ((f32[32,16,128]{2,1,0:T(8,128)}), f32[32,16,128]{2,1,0:T(8,128)S(1)}, u32[]{:S(2)}, u32[]{:S(2)}) async-start(f32[32,16,128]{2,1,0:T(8,128)} %pad_maximum_fusion), calls=%async_computation | async-start | bytes 524288 | tf_op jit(solution)/shard_map/all_to_all | solution.py:309
  14.1 0.8 %constant_dynamic-slice_fusion = f32[64,32]{1,0:T(8,128)S(1)} fusion(f32[64,2048]{1,0:T(8,128)} %rows_ref.1, s32[]{:T(128)S(6)} %select_n.20), kind=kLoop, calls=%fused_computation.3 | loop fusion | bytes 16388 | tf_op jit(solution)/shard_map/dynamic_slice | solution.py:311
  15.0 0.1 copy.7
  15.0 0.1 maximum_bitcast_fusion
  15.1 0.7 collective-permute-start.2
  15.8 0.7 collective-permute-start.1
  16.5 0.7 collective-permute-start
  17.1 0.0 collective-permute-done.2
  17.1 0.0 collective-permute-done.1
  17.2 0.0 collective-permute-done
  17.2 0.0 copy-start.1
  17.2 1.3 %collective-permute-start.3 = (f32[16,128]{1,0:T(8,128)S(1)}, f32[16,128]{1,0:T(8,128)S(1)}, u32[]{:S(2)}, u32[]{:S(2)}) collective-permute-start(f32[16,128]{1,0:T(8,128)S(1)} %add_select_fusion.look_ref), channel_id=1, source_target_pairs={{0,32},{64,96},{128,160},{192,224},{1,33},{65,97},{129,161},{193,2... | collective-permute-start | bytes 24584 | tf_op jit(solution)/shard_map/ppermute | solution.py:314
  18.5 7.9 %collective-permute-done.3.sent_ref = f32[16,128]{1,0:T(8,128)S(1)} collective-permute-done((f32[16,128]{1,0:T(8,128)S(1)}, f32[16,128]{1,0:T(8,128)S(1)}, u32[]{:S(2)}, u32[]{:S(2)}) %collective-permute-start.3) | collective-permute-done | bytes 8224 | tf_op jit(solution)/shard_map/ppermute | solution.py:314
  26.4 0.0 copy-start.2
  26.4 0.0 all-to-all-done
  26.4 0.0 copy-start
  26.4 0.0 copy-done.1
  26.5 0.6 copy-done.2
  27.0 0.1 copy-done
  27.2 39.9 %panel.1 = (f32[32,128]{1,0:T(8,128)}, f32[32,2048]{1,0:T(8,128)}, f32[32,2048]{1,0:T(8,128)}) custom-call(f32[512,128]{1,0:T(8,128)} %bitcast.9, f32[16,128]{1,0:T(8,128)} %copy-done.1, f32[16,128]{1,0:T(8,128)} %copy-done.2, f32[1,64]{1,0:T(1,128)} %bitcast.12, f32[64,2048]{1,0:T(8,128)} %rows_ref.1), custom_call_target="tpu_custom_call" | custom-call | tf_op jit(solution)/shard_map/panel/pallas_call | solution.py:281
  (4 shorter events, 0.1 us)
Async XLA Ops:
  2.2 24.2 %all-to-all-start = ((f32[32,16,128]{2,1,0:T(8,128)}), f32[32,16,128]{2,1,0:T(8,128)S(1)}, u32[]{:S(2)}, u32[]{:S(2)}) async-start(f32[32,16,128]{2,1,0:T(8,128)} %pad_maximum_fusion), calls=%async_computation | async-start | bytes 524288 | tf_op jit(solution)/shard_map/all_to_all | solution.py:309
  15.1 2.0 %collective-permute-start.2 = (f32[16,128]{1,0:T(8,128)S(1)}, f32[16,128]{1,0:T(8,128)S(1)}, u32[]{:S(2)}, u32[]{:S(2)}) collective-permute-start(f32[16,128]{1,0:T(8,128)S(1)} %maximum_bitcast_fusion), channel_id=1, source_target_pairs={{0,64},{1,65},{2,66},{3,67},{4,68},{5,69},{6,70},{7,71},{8,72},{9,... | collective-permute-start | bytes 24584 | tf_op jit(solution)/shard_map/ppermute | solution.py:312
  15.8 1.4 %collective-permute-start.1 = (f32[16,128]{1,0:T(8,128)S(1)}, f32[16,128]{1,0:T(8,128)S(1)}, u32[]{:S(2)}, u32[]{:S(2)}) collective-permute-start(f32[16,128]{1,0:T(8,128)S(1)} %maximum_bitcast_fusion), channel_id=1, source_target_pairs={{0,128},{1,129},{2,130},{3,131},{4,132},{5,133},{6,134},{7,135},{8... | collective-permute-start | bytes 24584 | tf_op jit(solution)/shard_map/ppermute | solution.py:312
  16.5 0.7 %collective-permute-start = (f32[16,128]{1,0:T(8,128)S(1)}, f32[16,128]{1,0:T(8,128)S(1)}, u32[]{:S(2)}, u32[]{:S(2)}) collective-permute-start(f32[16,128]{1,0:T(8,128)S(1)} %maximum_bitcast_fusion), channel_id=1, source_target_pairs={{0,192},{1,193},{2,194},{3,195},{4,196},{5,197},{6,198},{7,199},{8... | collective-permute-start | bytes 24584 | tf_op jit(solution)/shard_map/ppermute | solution.py:312
  17.2 9.3 %copy-start.1 = (f32[16,128]{1,0:T(8,128)}, f32[16,128]{1,0:T(8,128)S(1)}, u32[]{:S(2)}) copy-start(f32[16,128]{1,0:T(8,128)S(1)} %add_select_fusion.look_ref) | copy-start | bytes 24580
  17.2 9.2 %collective-permute-start.3 = (f32[16,128]{1,0:T(8,128)S(1)}, f32[16,128]{1,0:T(8,128)S(1)}, u32[]{:S(2)}, u32[]{:S(2)}) collective-permute-start(f32[16,128]{1,0:T(8,128)S(1)} %add_select_fusion.look_ref), channel_id=1, source_target_pairs={{0,32},{64,96},{128,160},{192,224},{1,33},{65,97},{129,161},{193,2... | collective-permute-start | bytes 24584 | tf_op jit(solution)/shard_map/ppermute | solution.py:314
  26.4 0.6 copy-start.2
  26.4 0.7 %copy-start = (f32[32,16,128]{2,1,0:T(8,128)}, f32[32,16,128]{2,1,0:T(8,128)S(1)}, u32[]{:S(2)}) copy-start(f32[32,16,128]{2,1,0:T(8,128)S(1)} %all-to-all-done) | copy-start | bytes 786436
